TPU v7x, 32 devices: a whole 2x2x4 slice. The times are simulated.
32 devices in a mesh: obs: 16 (over z, x, core), cell: 2 (over y).
Axes of the slice: x: 2, y: 2, z: 4, core: 2. Of those that a mesh axis runs over, the one named last changes fastest.
Arguments:
- flux_field: bfloat16 [2, 16, 64, 128], P('cell', 'obs'), may hold values from -6 to 6
- footprint: bfloat16 [256, 16, 128, 128], P('obs', 'cell'), may hold values from -0.125 to 0.125
- block_index: int32 [256, 16], P('obs', 'cell'), may hold values from 0 to 15
- tile_count: int32 [16], P('obs'), may hold values from 1 to 16, 128 in all
- sounding_week: int32 [256, 128], P('obs'), may hold values from 0 to 3
- member_ids: int32 [16], replicated, may hold values from 0 to 15, each once
- observed: float32 [256, 128], P('obs'), may hold values from -6 to 6
- perturb: bfloat16 [256, 16, 128], P('obs'), may hold values from -6 to 6
- obs_weight: float32 [256, 128], P('obs'), may hold values from 0.3 to 3
Outputs:
- gradient: float32 [2, 16, 64, 128], P('cell', 'obs')
- residual: bfloat16 [256, 16, 128], P('obs')
All inputs are finite; a program needn't handle non-finite values. No bound on the sum of `tile_count` on one device may be relied on, other than what follows from the above.
Results may differ from a plain program's by a relative error of at most 0.0028.
Values may be sent and summed in bfloat16 or wider, within the bound.
No kernel may reach another device: no remote copies, remote signals or barrier semaphores. Data moves between devices by JAX's collectives and lax.ppermute only.
A program may use at most 64 MiB of HBM per device.

v0:
```python
import jax
import jax.numpy as jnp
from jax import lax
from jax.sharding import PartitionSpec as P

MEMBERS = 16
WEEKS = 4


def weigh_misfit(modeled, alive, weights, seen, shifted):
    return (
        alive[:, None, None] * weights[:, None, :] * (modeled - seen[:, None, :] - shifted)
    ).astype(jnp.bfloat16)


def on_device(
    flux_field,
    footprint,
    block_index,
    tile_count,
    sounding_week,
    member_ids,
    observed,
    perturb,
    obs_weight,
):
    slab_rows = lax.all_gather(flux_field, "obs", axis=1, tiled=True)[0]
    slab_count = slab_rows.shape[0]
    slots = footprint.shape[0]
    sounds = footprint.shape[2]
    cells = footprint.shape[3]
    rows_all = WEEKS * MEMBERS
    chosen = slab_rows[block_index]
    mixing = jnp.einsum("tkrc,tksc->trs", chosen, footprint, preferred_element_type=jnp.float32)
    mixing = mixing.reshape(slots, WEEKS, MEMBERS, sounds)
    week_ids = jnp.arange(WEEKS, dtype=jnp.int32)
    week_hot = (sounding_week[:, None, :] == week_ids[None, :, None]).astype(jnp.float32)
    partial_value = jnp.einsum("twms,tws->tms", mixing, week_hot, precision=lax.Precision.HIGHEST)
    alive = (jnp.arange(slots, dtype=jnp.int32) < tile_count[0]).astype(jnp.float32)
    member_hot = (member_ids[:, None] == jnp.arange(MEMBERS, dtype=jnp.int32)[None, :]).astype(
        jnp.float32
    )
    shifted = jnp.einsum(
        "mk,tks->tms", member_hot, perturb.astype(jnp.float32), precision=lax.Precision.HIGHEST
    )
    modeled = lax.psum(partial_value, "cell")
    residual = weigh_misfit(modeled, alive, obs_weight, observed, shifted)
    week_mask = week_hot.astype(jnp.bfloat16)
    flat_blocks = block_index.reshape(-1)
    adjoint_rows = (residual[:, None, :, :] * week_mask[:, :, None, :]).reshape(
        slots, rows_all, sounds
    )
    contrib = jnp.einsum(
        "trs,tksc->tkrc", adjoint_rows, footprint, preferred_element_type=jnp.float32
    )
    partial_grad = jax.ops.segment_sum(
        contrib.reshape(-1, rows_all, cells), flat_blocks, num_segments=slab_count
    )
    gradient = lax.psum_scatter(partial_grad, "obs", scatter_dimension=0, tiled=True)
    return (gradient[None], residual)


def solution(mesh):
    return jax.shard_map(
        on_device,
        mesh=mesh,
        in_specs=(
            P("cell", "obs", None, None),
            P("obs", "cell", None, None),
            P("obs", "cell"),
            P("obs"),
            P("obs", None),
            P(),
            P("obs", None),
            P("obs", None, None),
            P("obs", None),
        ),
        out_specs=(P("cell", "obs", None, None), P("obs", None, None)),
        check_vma=False,
    )
```

profile of v0, /device:TPU:0, one launch (start us, length us, event | category | flops | bytes accessed | tf_op | source)
XLA Modules:
  0.0 140.4 jit_solution(12556074545440462448)
XLA Ops:
  7.2 0.0 copy-start
  7.2 0.0 all-reduce.2.cloned.1.call-start
  7.2 0.7 compare_select_fusion
  7.9 0.1 copy.17
  8.0 0.1 reshape.36
  8.1 0.7 fusion.4
  8.8 24.0 %all_gather.3 = bf16[1,16,64,128]{3,2,0,1:T(8,128)(2,1)S(1)} all-gather(bf16[1,1,64,128]{3,2,0,1:T(8,128)(2,1)} %bitcast.47), channel_id=1, replica_groups=mesh['obs'=16,'cell'=2] {'obs'}, dimensions={1}, use_global_device_ids=true | all-gather | bytes 278528 | tf_op jit(solution)/shard_map/all_gather | solution.py:27
  32.8 0.9 gather_fusion
  33.8 0.0 copy-start.3
  33.8 0.0 copy-start.5
  33.8 0.0 copy-start.4
  33.8 0.0 copy-start.6
  33.8 3.7 %fusion.8 = f32[16,64,128,1]{2,1,3,0:T(8,128)S(1)} fusion(bf16[16,8,64,128]{3,2,1,0:T(8,128)(2,1)S(1)} %bitcast.43, bf16[16,8,128,128]{3,2,1,0:T(8,128)(2,1)} %param.10), kind=kOutput, calls=%fused_computation.19 | convolution fusion | flops 268435456 | bytes 6815744 | tf_op jit(solution)/shard_map/tkrc,tksc->trs/dot_general | solution.py:34
  37.6 0.7 multiply_reduce_fusion
  38.3 0.0 all-reduce.2.cloned.1.call-update
  38.3 0.0 reduce-scatter.2.cloned.1.call-start
  38.3 0.0 copy-done.3
  38.4 0.1 copy.15
  39.1 0.1 reshape.44
  39.2 0.0 copy-done.5
  39.2 0.1 broadcast_multiply_fusion.1
  39.3 17.9 %all-reduce.2.cloned.1.call-done = f32[16,16,128]{2,1,0:T(8,128)} async-done(((f32[16,16,128]{2,1,0:T(8,128)}), f32[16,16,128]{2,1,0:T(8,128)}) %all-reduce.2.cloned.1.call-update) | async-done | bytes 131088 | tf_op jit(solution)/shard_map/psum | solution.py:46
  57.2 0.0 copy-done
  57.2 0.0 copy-done.4
  57.2 0.0 copy-done.6
  57.2 1.1 fusion.2
  58.3 0.0 copy-start.2
  58.4 4.8 %fusion.9 = f32[16,64,8,128]{3,1,2,0:T(8,128)} fusion(bf16[16,64,128,1]{2,1,3,0:T(8,128)(2,1)S(1)} %bitcast.45, bf16[16,8,128,128]{3,2,1,0:T(8,128)(2,1)} %param.10), kind=kOutput, calls=%fused_computation.20 | convolution fusion | flops 268435456 | bytes 8650752 | tf_op jit(solution)/shard_map/trs,tksc->tkrc/dot_general | solution.py:53
  63.2 0.0 copy-done.2
  63.3 13.5 %scatter_fusion = f32[16,64,128]{2,1,0:T(8,128)S(1)} fusion(f32[16,64,128]{2,1,0:T(8,128)S(1)} %broadcast_in_dim.6, s32[128]{0:T(128)S(1)} %reshape.44, f32[128,64,128]{2,1,0:T(8,128)} %bitcast.42), kind=kCustom, calls=%fused_computation.1 | custom fusion | flops 1048576 | bytes 12583424 | tf_op jit(solution)/shard_map/scatter-add | solution.py:56
  76.8 0.0 copy-start.1
  76.8 0.8 copy-done.1
  77.6 0.0 reduce-scatter.2.cloned.1.call-update
  77.6 55.9 %reduce-scatter.2.cloned.1.call-done = f32[1,64,128]{2,1,0:T(8,128)} async-done(((f32[16,64,128]{2,1,0:T(8,128)}), f32[1,64,128]{2,1,0:T(8,128)}) %reduce-scatter.2.cloned.1.call-update) | async-done | bytes 32784 | tf_op jit(solution)/shard_map/reduce_scatter | solution.py:59
  (4 shorter events, 0.1 us)
Async XLA Ops:
  7.2 50.0 %copy-start = (bf16[16,16,128]{2,1,0:T(8,128)(2,1)S(1)}, bf16[16,16,128]{2,1,0:T(8,128)(2,1)}, u32[]{:S(2)}) copy-start(bf16[16,16,128]{2,1,0:T(8,128)(2,1)} %param.16) | copy-start | bytes 196612
  7.2 50.0 %all-reduce.2.cloned.1.call-start = ((), (), s32[]{:S(2)}) async-start(), calls=%async_computation.1 | async-start | bytes 262144 | tf_op jit(solution)/shard_map/psum | solution.py:46
  33.8 4.6 %copy-start.3 = (s32[16,8]{0,1:T(8,128)S(1)}, s32[16,8]{0,1:T(8,128)}, u32[]{:S(2)}) copy-start(s32[16,8]{0,1:T(8,128)} %param.11) | copy-start | bytes 1540
  33.8 5.4 %copy-start.5 = (f32[16,128]{1,0:T(8,128)S(1)}, f32[16,128]{1,0:T(8,128)}, u32[]{:S(2)}) copy-start(f32[16,128]{1,0:T(8,128)} %param.17) | copy-start | bytes 24580
  33.8 23.4 %copy-start.4 = (f32[16,128]{1,0:T(8,128)S(1)}, f32[16,128]{1,0:T(8,128)}, u32[]{:S(2)}) copy-start(f32[16,128]{1,0:T(8,128)} %param.15) | copy-start | bytes 24580
  33.8 23.4 %copy-start.6 = (s32[16]{0:T(128)S(1)}, s32[16]{0:T(128)}, u32[]{:S(2)}) copy-start(s32[16]{0:T(128)} %param.14) | copy-start | bytes 196
  38.3 95.2 %reduce-scatter.2.cloned.1.call-start = ((), (), s32[]{:S(2)}) async-start(), calls=%async_computation.2 | async-start | bytes 557056 | tf_op jit(solution)/shard_map/reduce_scatter | solution.py:59
  58.3 4.9 %copy-start.2 = (bf16[16,16,128]{2,1,0:T(8,128)(2,1)}, bf16[16,16,128]{2,1,0:T(8,128)(2,1)S(1)}, u32[]{:S(2)}) copy-start(bf16[16,16,128]{2,1,0:T(8,128)(2,1)S(1)} %fusion.2) | copy-start | bytes 196612
  76.8 0.8 copy-start.1
Sparse Core Ops, SparseCore 0:
  38.4 18.7 all-reduce.1
  77.7 55.7 reduce-scatter.1
where the time goes:
time: 141 us; the launch traced here: 140 us
  waiting for transfers between devices  73.9 us (52%)
  blocking collectives  24 us (17%)
  other arithmetic  15.7 us (11%)
  between operations  14.8 us (10%)
  matrix products  9.68 us (7%)
  local copies, waits for them, and re-layouts  2.14 us (2%)
    reduce_scatter x1, waiting for transfers between devices, on_device(): lax.psum_scatter(partial_grad, 'obs', scatter_dimension=0, tiled=True)  55.9 us
    all_gather x1, blocking collectives, on_device(): slab_rows = lax.all_gather(flux_field, 'obs', axis=1, tiled=True)[0]  24 us
    psum x1, waiting for transfers between devices, on_device(): modeled = lax.psum(partial_value, 'cell')  17.9 us
    scatter-add x1, other arithmetic, on_device(): jax.ops.segment_sum(contrib.reshape(-1, rows_all, cells), flat_blocks, nu...  13.5 us
    dot_general x1, matrix products, on_device(): jnp.einsum('trs,tksc->tkrc', adjoint_rows, footprint, preferred_element_t...  4.84 us
    dot_general x1, matrix products, on_device(): jnp.einsum('tkrc,tksc->trs', chosen, footprint, preferred_element_type=jn...  3.73 us
  transfers between devices with their start and end apart: 2, of which 2 were waited for; matrix products, arithmetic and copies ran while one was open for 0% of the time, Pallas kernels for 0%

commit v1 on v0

v1 whole, which is shorter than its diff:
```python
import functools

import jax
import jax.numpy as jnp
from jax import lax
from jax.experimental import pallas as pl
from jax.experimental.pallas import tpu as pltpu
from jax.sharding import PartitionSpec as P

MEMBERS = 16
WEEKS = 4
ROWS = WEEKS * MEMBERS

VMEM = pl.BlockSpec(memory_space=pltpu.VMEM)
SMEM = pl.BlockSpec(memory_space=pltpu.SMEM)


def phases_of(count):
    bits = [1 << i for i in range(count.bit_length() - 1)]
    upper = bits[:0:-1]
    rounds = [upper[:1]] if len(upper) % 2 else []
    rest = upper[len(upper) % 2 :]
    rounds += [rest[i : i + 2] for i in range(0, len(rest), 2)]
    return rounds + [bits[:1]]


def masks_of(bits):
    masks = [0]
    for bit in bits:
        masks += [mask | bit for mask in masks]
    return masks


def order_of(rounds):
    order = [0]
    for bits in rounds:
        order = [mask | low for mask in masks_of(bits) for low in order]
    return order


def swap(value, axis, count, mask):
    return lax.ppermute(value, axis, [(i, i ^ mask) for i in range(count)])


def place_of(diff, rounds):
    order = order_of(rounds)
    place = jnp.int32(0)
    for bit in [b for bits in rounds for b in bits]:
        step = order.index(bit)
        place = place + ((diff // bit) % 2) * step
    return place


def forward_kernel(rounds, blocks_ref, weeks_ref, mine_ref, other_ref, print_ref, out_ref, flux_ref):
    me = lax.axis_index("obs")
    half = mine_ref.shape[0]
    flux_ref[:half] = mine_ref[...]
    flux_ref[half:] = other_ref[...]
    slots, per_tile = print_ref.shape[:2]
    for tile in range(slots):
        total = None
        for j in range(0, per_tile, 2):
            first = place_of(blocks_ref[tile, j] ^ me, rounds)
            second = place_of(blocks_ref[tile, j + 1] ^ me, rounds)
            rows = jnp.concatenate([flux_ref[first], flux_ref[second]], axis=1)
            sens = jnp.concatenate([print_ref[tile, j], print_ref[tile, j + 1]], axis=1)
            part = lax.dot_general(
                rows, sens, (((1,), (1,)), ((), ())), preferred_element_type=jnp.float32
            )
            total = part if total is None else total + part
        weeks = weeks_ref[pl.ds(tile, 1), :]
        picked = total[:MEMBERS]
        for week in range(1, WEEKS):
            picked = jnp.where(weeks == week, total[week * MEMBERS : (week + 1) * MEMBERS], picked)
        out_ref[tile] = picked


def adjoint_kernel(
    rounds,
    blocks_ref,
    count_ref,
    ids_ref,
    weeks_ref,
    own_ref,
    far_ref,
    seen_ref,
    noise_ref,
    weight_ref,
    print_ref,
    keep_ref,
    send_ref,
    residual_ref,
    grad_ref,
):
    me = lax.axis_index("obs")
    slots, per_tile = print_ref.shape[:2]
    grad_ref[...] = jnp.zeros_like(grad_ref)
    count = count_ref[0]
    member = lax.broadcasted_iota(jnp.int32, (MEMBERS, MEMBERS), 1)
    row = lax.broadcasted_iota(jnp.int32, (MEMBERS, MEMBERS), 0)
    chosen = jnp.zeros((MEMBERS, MEMBERS), jnp.int32)
    for m in range(MEMBERS):
        chosen = jnp.where(row == m, ids_ref[m], chosen)
    hot = (member == chosen).astype(jnp.float32).astype(jnp.bfloat16)
    for tile in range(slots):
        shifted = jnp.dot(hot, noise_ref[tile], preferred_element_type=jnp.float32)
        alive = jnp.where(tile < count, jnp.float32(1), jnp.float32(0))
        weights = alive * weight_ref[pl.ds(tile, 1), :]
        seen = seen_ref[pl.ds(tile, 1), :]
        modeled = own_ref[tile] + far_ref[tile]
        residual = weights * (modeled - seen - shifted)
        residual_ref[tile] = residual.astype(jnp.bfloat16)
        weeks = weeks_ref[pl.ds(tile, 1), :]
        rows = jnp.concatenate(
            [jnp.where(weeks == week, residual, 0.0) for week in range(WEEKS)], axis=0
        ).astype(jnp.bfloat16)
        for j in range(0, per_tile, 2):
            first = place_of(blocks_ref[tile, j] ^ me, rounds)
            second = place_of(blocks_ref[tile, j + 1] ^ me, rounds)
            sens = jnp.concatenate([print_ref[tile, j], print_ref[tile, j + 1]], axis=1)
            part = jnp.dot(rows, sens, preferred_element_type=jnp.float32)
            cells = part.shape[1] // 2
            grad_ref[first] += part[:, :cells]
            grad_ref[second] += part[:, cells:]
    half = keep_ref.shape[0]
    keep_ref[...] = grad_ref[:half]
    send_ref[...] = grad_ref[half:]


def on_device(
    devices,
    slabs,
    flux_field,
    footprint,
    block_index,
    tile_count,
    sounding_week,
    member_ids,
    observed,
    perturb,
    obs_weight,
):
    rounds = phases_of(devices)
    slots, per_tile, sounds, cells = footprint.shape
    half = devices // 2
    params = pltpu.CompilerParams(vmem_limit_bytes=24 << 20)

    have = flux_field[0]
    for bits in rounds[:-1]:
        have = jnp.concatenate([have] + [swap(have, "obs", devices, m) for m in masks_of(bits)[1:]], axis=0)
    other = swap(have, "obs", devices, rounds[-1][0])
    modeled = pl.pallas_call(
        functools.partial(forward_kernel, rounds),
        out_shape=jax.ShapeDtypeStruct((slots, MEMBERS, sounds), jnp.float32),
        in_specs=[SMEM, VMEM, VMEM, VMEM, VMEM],
        out_specs=VMEM,
        scratch_shapes=[pltpu.VMEM((devices, ROWS, cells), jnp.bfloat16)],
        compiler_params=params,
        name="forward",
    )(block_index, sounding_week, have, other, footprint)
    mask = 1
    while 2 * mask < slabs:
        modeled = modeled + swap(modeled, "cell", slabs, mask)
        mask *= 2
    far = swap(modeled, "cell", slabs, mask)
    keep, send, residual = pl.pallas_call(
        functools.partial(adjoint_kernel, rounds),
        out_shape=(
            jax.ShapeDtypeStruct((half, ROWS, cells), jnp.float32),
            jax.ShapeDtypeStruct((half, ROWS, cells), jnp.float32),
            jax.ShapeDtypeStruct((slots, MEMBERS, sounds), jnp.bfloat16),
        ),
        in_specs=[SMEM, SMEM, SMEM] + [VMEM] * 7,
        out_specs=(VMEM, VMEM, VMEM),
        scratch_shapes=[pltpu.VMEM((devices, ROWS, cells), jnp.float32)],
        compiler_params=params,
        name="adjoint",
    )(
        block_index,
        tile_count,
        member_ids,
        sounding_week,
        modeled,
        far,
        observed,
        perturb,
        obs_weight,
        footprint,
    )
    total = keep + swap(send, "obs", devices, rounds[-1][0])
    for bits in rounds[-2::-1]:
        masks = masks_of(bits)
        pieces = jnp.split(total, len(masks), axis=0)
        total = pieces[0]
        for mask, piece in zip(masks[1:], pieces[1:]):
            total = total + swap(piece, "obs", devices, mask)
    return (total[None], residual)


def solution(mesh):
    devices, slabs = mesh.shape["obs"], mesh.shape["cell"]
    return jax.shard_map(
        functools.partial(on_device, devices, slabs),
        mesh=mesh,
        in_specs=(
            P("cell", "obs", None, None),
            P("obs", "cell", None, None),
            P("obs", "cell"),
            P("obs"),
            P("obs", None),
            P(),
            P("obs", None),
            P("obs", None, None),
            P("obs", None),
        ),
        out_specs=(P("cell", "obs", None, None), P("obs", None, None)),
        check_vma=False,
    )
```

time: 141 us -> 48.4 us (0.34)
  waiting for transfers between devices: 73.9 us -> 17 us
  blocking collectives: 24 us -> 0 us
  starting transfers between devices: 0.08 us -> 15.5 us
  other arithmetic: 15.7 us -> 1.39 us
  between operations: 14.8 us -> 1.41 us
  matrix products: 9.68 us -> 0 us
  Pallas kernels: 0 us -> 8.16 us
  local copies, waits for them, and re-layouts: 2.14 us -> 4.48 us
    reduce_scatter x1 -> x0, waiting for transfers between devices: 55.9 us -> none  [on_device(): lax.psum_scatter(partial_grad, 'obs', scatter_dimension=0, tiled=True)]
    all_gather x1 -> x0, blocking collectives: 24 us -> none  [on_device(): slab_rows = lax.all_gather(flux_field, 'obs', axis=1, tiled=True)[0]]
    psum x1 -> x0, waiting for transfers between devices: 17.9 us -> none  [on_device(): modeled = lax.psum(partial_value, 'cell')]
    ppermute x0 -> x11, waiting for transfers between devices: none -> 17 us  [swap(): return lax.ppermute(value, axis, [(i, i ^ mask) for i in range(count)])]
    ppermute x0 -> x11, starting transfers between devices: none -> 15.5 us  [swap(): return lax.ppermute(value, axis, [(i, i ^ mask) for i in range(count)])]
    scatter-add x1 -> x0, other arithmetic: 13.5 us -> none  [on_device(): jax.ops.segment_sum(contrib.reshape(-1, rows_all, cells), flat_blocks, nu...]
    dot_general x3 -> x0, matrix products: 9.68 us -> none  [the longest x1 4.84 us: on_device(): jnp.einsum('trs,tksc->tkrc', adjoint_rows, footprint, preferred_element_t...]
    pallas_call x0 -> x2, Pallas kernels: none -> 8.16 us  [the longest x1 4.81 us: on_device(): pl.pallas_call(functools.partial(adjoint_kernel, rounds), out_shape=(jax....]
  transfers between devices with their start and end apart: 2 -> 11, of which waited for: 2 -> 9; matrix products, arithmetic and copies ran while one was open for 0% -> 3% of each run, Pallas kernels for 0% -> 0%
where the time goes in v1:
time: 48.4 us; the launch traced here: 47.9 us
  waiting for transfers between devices  17 us (35%)
  starting transfers between devices  15.5 us (32%)
  Pallas kernels  8.16 us (17%)
  local copies, waits for them, and re-layouts  4.48 us (9%)
  between operations  1.41 us (3%)
  other arithmetic  1.39 us (3%)
    ppermute x11, waiting for transfers between devices, swap(): return lax.ppermute(value, axis, [(i, i ^ mask) for i in range(count)])  17 us
    ppermute x11, starting transfers between devices, swap(): return lax.ppermute(value, axis, [(i, i ^ mask) for i in range(count)])  15.5 us
    pallas_call x1, Pallas kernels, on_device(): pl.pallas_call(functools.partial(adjoint_kernel, rounds), out_shape=(jax....  4.81 us
    unnamed x19, local copies, waits for them, and re-layouts  4.45 us
    pallas_call x1, Pallas kernels, on_device(): pl.pallas_call(functools.partial(forward_kernel, rounds), out_shape=jax.S...  3.35 us
  transfers between devices with their start and end apart: 11, of which 9 were waited for; matrix products, arithmetic and copies ran while one was open for 3% of the time, Pallas kernels for 0%

profile of v1, /device:TPU:0, one launch (start us, length us, event | category | flops | bytes accessed | tf_op | source)
XLA Modules:
  0.0 47.9 jit_solution(2679330793821880126)
XLA Ops:
  0.6 0.0 copy-start.5
  0.6 0.0 copy-start.2
  0.7 0.0 copy-start.4
  0.7 0.0 copy-start.6
  0.7 4.1 %collective-permute-start = (bf16[1,64,128]{2,1,0:T(8,128)(2,1)}, bf16[1,64,128]{2,1,0:T(8,128)(2,1)S(1)}, u32[]{:S(2)}, u32[]{:S(2)}) collective-permute-start(bf16[1,64,128]{2,1,0:T(8,128)(2,1)} %bitcast.4), channel_id=1, source_target_pairs={{0,16},{2,18},{4,20},{6,22},{8,24},{10,26},{12,28},{14,30},{16,0},... | collective-permute-start | bytes 49160 | tf_op jit(solution)/shard_map/ppermute | solution.py:42
  4.8 0.8 %constant_dynamic-update-slice_fusion.4 = bf16[8,64,128]{2,1,0:T(8,128)(2,1)S(1)} fusion(bf16[1,1,64,128]{3,2,1,0:T(8,128)(2,1)} %param.9), kind=kLoop, calls=%fused_computation.10 | loop fusion | bytes 32768
  5.5 1.2 %collective-permute-done = bf16[1,64,128]{2,1,0:T(8,128)(2,1)S(1)} collective-permute-done((bf16[1,64,128]{2,1,0:T(8,128)(2,1)}, bf16[1,64,128]{2,1,0:T(8,128)(2,1)S(1)}, u32[]{:S(2)}, u32[]{:S(2)}) %collective-permute-start) | collective-permute-done | bytes 16416 | tf_op jit(solution)/shard_map/ppermute | solution.py:42
  6.7 0.7 %pad_maximum_fusion = bf16[2,64,128]{2,1,0:T(8,128)(2,1)S(1)} fusion(bf16[1,64,128]{2,1,0:T(8,128)(2,1)S(1)} %collective-permute-done, bf16[1,64,128]{2,1,0:T(8,128)(2,1)} %bitcast.5), kind=kLoop, calls=%fused_computation.5 | loop fusion | flops 16384 | bytes 65536 | tf_op jit(solution)/shard_map/concatenate | solution.py:150
  7.4 2.8 %collective-permute-start.3 = (bf16[2,64,128]{2,1,0:T(8,128)(2,1)S(1)}, bf16[2,64,128]{2,1,0:T(8,128)(2,1)S(1)}, u32[]{:S(2)}, u32[]{:S(2)}) collective-permute-start(bf16[2,64,128]{2,1,0:T(8,128)(2,1)S(1)} %pad_maximum_fusion), channel_id=1, source_target_pairs={{0,12},{2,14},{4,8},{6,10},{8,4},{10,6},{12,0},{14,2},{16,28},{18,... | collective-permute-start | bytes 98312 | tf_op jit(solution)/shard_map/ppermute | solution.py:42
  10.3 0.5 %collective-permute-start.2 = (bf16[2,64,128]{2,1,0:T(8,128)(2,1)S(1)}, bf16[2,64,128]{2,1,0:T(8,128)(2,1)S(1)}, u32[]{:S(2)}, u32[]{:S(2)}) collective-permute-start(bf16[2,64,128]{2,1,0:T(8,128)(2,1)S(1)} %pad_maximum_fusion), channel_id=1, source_target_pairs={{0,4},{2,6},{4,0},{6,2},{8,12},{10,14},{12,8},{14,10},{16,20},{18,... | collective-permute-start | bytes 98312 | tf_op jit(solution)/shard_map/ppermute | solution.py:42
  10.8 0.1 collective-permute-start.1
  10.9 3.8 %collective-permute-done.1 = bf16[2,64,128]{2,1,0:T(8,128)(2,1)S(1)} collective-permute-done((bf16[2,64,128]{2,1,0:T(8,128)(2,1)S(1)}, bf16[2,64,128]{2,1,0:T(8,128)(2,1)S(1)}, u32[]{:S(2)}, u32[]{:S(2)}) %collective-permute-start.1) | collective-permute-done | bytes 32800 | tf_op jit(solution)/shard_map/ppermute | solution.py:42
  14.7 0.0 collective-permute-done.2
  14.7 0.0 collective-permute-done.3
  14.8 0.1 collective-permute-start.4
  14.8 0.8 %copy.12.blocks_ref = s32[16,8]{1,0:T(8,128)S(1)} copy(s32[16,8]{0,1:T(8,128)} %param.11) | data formatting | bytes 1024 | tf_op args[2]
  15.6 0.6 %collective-permute-done.4.other_ref = bf16[8,64,128]{2,1,0:T(8,128)(2,1)S(1)} collective-permute-done((bf16[8,64,128]{2,1,0:T(8,128)(2,1)S(1)}, bf16[8,64,128]{2,1,0:T(8,128)(2,1)S(1)}, u32[]{:S(2)}, u32[]{:S(2)}) %collective-permute-start.4) | collective-permute-done | bytes 131104 | tf_op jit(solution)/shard_map/ppermute | solution.py:42
  16.2 0.0 copy-start
  16.2 2.2 %copy-done = bf16[16,8,128,128]{3,2,1,0:T(8,128)(2,1)S(1)} copy-done((bf16[16,8,128,128]{3,2,1,0:T(8,128)(2,1)S(1)}, bf16[16,8,128,128]{3,2,1,0:T(8,128)(2,1)}, u32[]{:S(2)}) %copy-start) | copy-done | bytes 4194328
  18.4 0.0 copy-start.3
  18.4 0.7 %copy-done.3 = s32[16,128]{1,0:T(8,128)S(1)} copy-done((s32[16,128]{1,0:T(8,128)S(1)}, s32[16,128]{1,0:T(8,128)}, u32[]{:S(2)}) %copy-start.3) | copy-done | bytes 8216
  19.1 0.0 copy-start.1
  19.1 3.4 %forward.1.own_ref = f32[16,16,128]{2,1,0:T(8,128)S(1)} custom-call(s32[16,8]{1,0:T(8,128)S(1)} %copy.12.blocks_ref, s32[16,128]{1,0:T(8,128)S(1)} %copy-done.3, bf16[8,64,128]{2,1,0:T(8,128)(2,1)S(1)} %constant_dynamic-update-slice_fusion.mine_ref, bf16[8,64,128]{2,1,0:T(8,128)(2,1)S(1)} %collective-permute-done.4.other_ref, ...), custom_call_target="tpu_custom_call" | custom-call | tf_op jit(solution)/shard_map/forward/pallas_call | solution.py:152
  22.4 1.6 %collective-permute-start.5 = (f32[16,16,128]{2,1,0:T(8,128)S(1)}, f32[16,16,128]{2,1,0:T(8,128)S(1)}, u32[]{:S(2)}, u32[]{:S(2)}) collective-permute-start(f32[16,16,128]{2,1,0:T(8,128)S(1)} %forward.1.own_ref), channel_id=1, source_target_pairs={{0,1},{1,0},{2,3},{3,2},{4,5},{5,4},{6,7},{7,6},{8,9},{9,8},{10,11... | collective-permute-start | bytes 393224 | tf_op jit(solution)/shard_map/ppermute | solution.py:42
  24.7 3.4 %collective-permute-done.5.far_ref = f32[16,16,128]{2,1,0:T(8,128)S(1)} collective-permute-done((f32[16,16,128]{2,1,0:T(8,128)S(1)}, f32[16,16,128]{2,1,0:T(8,128)S(1)}, u32[]{:S(2)}, u32[]{:S(2)}) %collective-permute-start.5) | collective-permute-done | bytes 131104 | tf_op jit(solution)/shard_map/ppermute | solution.py:42
  28.0 0.0 copy-done.5
  28.0 0.0 copy-done.2
  28.0 0.0 copy-done.4
  28.1 0.0 copy-done.6
  28.1 0.0 copy-done.1
  28.1 4.8 %adjoint.1 = (f32[8,64,128]{2,1,0:T(8,128)S(1)}, f32[8,64,128]{2,1,0:T(8,128)S(1)}, bf16[16,16,128]{2,1,0:T(8,128)(2,1)}) custom-call(s32[16,8]{1,0:T(8,128)S(1)} %copy.12.blocks_ref, s32[1]{0:T(128)S(6)} %copy.17.count_ref, s32[16]{0:T(128)S(1)} %copy-done.6, s32[16,128]{1,0:T(8,128)S(1)} %copy-done.3, f32[16,16,128]{2,1,0:T(8,128)S(1)} %forward.1.own_ref, ...), custom_call_target="tpu_custom_call" | custom-call | tf_op jit(solution)/shard_map/adjoint/pallas_call | solution.py:166
  32.9 0.0 collective-permute-start.6
  32.9 1.5 %collective-permute-done.6 = f32[8,64,128]{2,1,0:T(8,128)S(1)} collective-permute-done((f32[8,64,128]{2,1,0:T(8,128)S(1)}, f32[8,64,128]{2,1,0:T(8,128)S(1)}, u32[]{:S(2)}, u32[]{:S(2)}) %collective-permute-start.6) | collective-permute-done | bytes 262176 | tf_op jit(solution)/shard_map/ppermute | solution.py:42
  34.5 0.4 collective-permute-start.7
  34.8 2.7 %collective-permute-start.9 = (f32[2,64,128]{2,1,0:T(8,128)S(1)}, f32[2,64,128]{2,1,0:T(8,128)S(1)}, u32[]{:S(2)}, u32[]{:S(2)}) collective-permute-start(f32[2,64,128]{2,1,0:T(8,128)S(1)} %get-tuple-element.9), channel_id=1, source_target_pairs={{0,12},{2,14},{4,8},{6,10},{8,4},{10,6},{12,0},{14,2},{16,28},{18,... | collective-permute-start | bytes 196616 | tf_op jit(solution)/shard_map/ppermute | solution.py:42
  37.5 0.5 %collective-permute-start.8 = (f32[2,64,128]{2,1,0:T(8,128)S(1)}, f32[2,64,128]{2,1,0:T(8,128)S(1)}, u32[]{:S(2)}, u32[]{:S(2)}) collective-permute-start(f32[2,64,128]{2,1,0:T(8,128)S(1)} %get-tuple-element.10), channel_id=1, source_target_pairs={{0,4},{2,6},{4,0},{6,2},{8,12},{10,14},{12,8},{14,10},{16,20},{18,... | collective-permute-start | bytes 196616 | tf_op jit(solution)/shard_map/ppermute | solution.py:42
  38.0 1.2 %collective-permute-done.7 = f32[2,64,128]{2,1,0:T(8,128)S(1)} collective-permute-done((f32[2,64,128]{2,1,0:T(8,128)S(1)}, f32[2,64,128]{2,1,0:T(8,128)S(1)}, u32[]{:S(2)}, u32[]{:S(2)}) %collective-permute-start.7) | collective-permute-done | bytes 65568 | tf_op jit(solution)/shard_map/ppermute | solution.py:42
  39.2 1.9 %collective-permute-done.9 = f32[2,64,128]{2,1,0:T(8,128)S(1)} collective-permute-done((f32[2,64,128]{2,1,0:T(8,128)S(1)}, f32[2,64,128]{2,1,0:T(8,128)S(1)}, u32[]{:S(2)}, u32[]{:S(2)}) %collective-permute-start.9) | collective-permute-done | bytes 65568 | tf_op jit(solution)/shard_map/ppermute | solution.py:42
  41.1 0.9 %collective-permute-done.8 = f32[2,64,128]{2,1,0:T(8,128)S(1)} collective-permute-done((f32[2,64,128]{2,1,0:T(8,128)S(1)}, f32[2,64,128]{2,1,0:T(8,128)S(1)}, u32[]{:S(2)}, u32[]{:S(2)}) %collective-permute-start.8) | collective-permute-done | bytes 65568 | tf_op jit(solution)/shard_map/ppermute | solution.py:42
  42.1 2.7 %collective-permute-start.10 = (f32[1,64,128]{2,1,0:T(8,128)S(1)}, f32[1,64,128]{2,1,0:T(8,128)S(1)}, u32[]{:S(2)}, u32[]{:S(2)}) collective-permute-start(f32[1,64,128]{2,1,0:T(8,128)S(1)} %split.29), channel_id=1, source_target_pairs={{0,16},{2,18},{4,20},{6,22},{8,24},{10,26},{12,28},{14,30},{16,0},... | collective-permute-start | bytes 98312 | tf_op jit(solution)/shard_map/ppermute | solution.py:42
  44.8 2.5 %collective-permute-done.10 = f32[1,64,128]{2,1,0:T(8,128)S(1)} collective-permute-done((f32[1,64,128]{2,1,0:T(8,128)S(1)}, f32[1,64,128]{2,1,0:T(8,128)S(1)}, u32[]{:S(2)}, u32[]{:S(2)}) %collective-permute-start.10) | collective-permute-done | bytes 32800 | tf_op jit(solution)/shard_map/ppermute | solution.py:42
  47.3 0.6 %fusion.2 = f32[1,1,64,128]{3,2,1,0:T(8,128)} fusion(f32[1,64,128]{2,1,0:T(8,128)S(1)} %collective-permute-done.10, f32[2,64,128]{2,1,0:T(8,128)S(1)} %fusion.1), kind=kLoop, calls=%fused_computation.4 | loop fusion | flops 8192 | bytes 98304 | tf_op jit(solution)/shard_map/broadcast_in_dim | solution.py:197
  (8 shorter events, 0.1 us)
Async XLA Ops:
  0.6 27.4 %copy-start.5 = (f32[16,128]{1,0:T(8,128)S(1)}, f32[16,128]{1,0:T(8,128)}, u32[]{:S(2)}) copy-start(f32[16,128]{1,0:T(8,128)} %weight_ref.1) | copy-start | bytes 24580
  0.6 27.4 %copy-start.2 = (bf16[16,16,128]{2,1,0:T(8,128)(2,1)S(1)}, bf16[16,16,128]{2,1,0:T(8,128)(2,1)}, u32[]{:S(2)}) copy-start(bf16[16,16,128]{2,1,0:T(8,128)(2,1)} %noise_ref.1) | copy-start | bytes 196612
  0.7 27.4 %copy-start.4 = (f32[16,128]{1,0:T(8,128)S(1)}, f32[16,128]{1,0:T(8,128)}, u32[]{:S(2)}) copy-start(f32[16,128]{1,0:T(8,128)} %seen_ref.1) | copy-start | bytes 24580
  0.7 27.4 %copy-start.6 = (s32[16]{0:T(128)S(1)}, s32[16]{0:T(128)}, u32[]{:S(2)}) copy-start(s32[16]{0:T(128)} %ids_ref.1) | copy-start | bytes 196
  0.7 6.0 %collective-permute-start = (bf16[1,64,128]{2,1,0:T(8,128)(2,1)}, bf16[1,64,128]{2,1,0:T(8,128)(2,1)S(1)}, u32[]{:S(2)}, u32[]{:S(2)}) collective-permute-start(bf16[1,64,128]{2,1,0:T(8,128)(2,1)} %bitcast.4), channel_id=1, source_target_pairs={{0,16},{2,18},{4,20},{6,22},{8,24},{10,26},{12,28},{14,30},{16,0},... | collective-permute-start | bytes 49160 | tf_op jit(solution)/shard_map/ppermute | solution.py:42
  7.4 7.3 %collective-permute-start.3 = (bf16[2,64,128]{2,1,0:T(8,128)(2,1)S(1)}, bf16[2,64,128]{2,1,0:T(8,128)(2,1)S(1)}, u32[]{:S(2)}, u32[]{:S(2)}) collective-permute-start(bf16[2,64,128]{2,1,0:T(8,128)(2,1)S(1)} %pad_maximum_fusion), channel_id=1, source_target_pairs={{0,12},{2,14},{4,8},{6,10},{8,4},{10,6},{12,0},{14,2},{16,28},{18,... | collective-permute-start | bytes 98312 | tf_op jit(solution)/shard_map/ppermute | solution.py:42
  10.3 4.5 %collective-permute-start.2 = (bf16[2,64,128]{2,1,0:T(8,128)(2,1)S(1)}, bf16[2,64,128]{2,1,0:T(8,128)(2,1)S(1)}, u32[]{:S(2)}, u32[]{:S(2)}) collective-permute-start(bf16[2,64,128]{2,1,0:T(8,128)(2,1)S(1)} %pad_maximum_fusion), channel_id=1, source_target_pairs={{0,4},{2,6},{4,0},{6,2},{8,12},{10,14},{12,8},{14,10},{16,20},{18,... | collective-permute-start | bytes 98312 | tf_op jit(solution)/shard_map/ppermute | solution.py:42
  10.8 3.9 %collective-permute-start.1 = (bf16[2,64,128]{2,1,0:T(8,128)(2,1)S(1)}, bf16[2,64,128]{2,1,0:T(8,128)(2,1)S(1)}, u32[]{:S(2)}, u32[]{:S(2)}) collective-permute-start(bf16[2,64,128]{2,1,0:T(8,128)(2,1)S(1)} %pad_maximum_fusion), channel_id=1, source_target_pairs={{0,8},{2,10},{4,12},{6,14},{8,0},{10,2},{12,4},{14,6},{16,24},{18,... | collective-permute-start | bytes 98312 | tf_op jit(solution)/shard_map/ppermute | solution.py:42
  14.8 1.4 %collective-permute-start.4 = (bf16[8,64,128]{2,1,0:T(8,128)(2,1)S(1)}, bf16[8,64,128]{2,1,0:T(8,128)(2,1)S(1)}, u32[]{:S(2)}, u32[]{:S(2)}) collective-permute-start(bf16[8,64,128]{2,1,0:T(8,128)(2,1)S(1)} %constant_dynamic-update-slice_fusion.mine_ref), channel_id=1, source_target_pairs={{0,2},{2,0},{4,6},{6,4},{8,10},{10,8},{12,14},{14,12},{16,18},{18,... | collective-permute-start | bytes 393224 | tf_op jit(solution)/shard_map/ppermute | solution.py:42
  16.2 2.2 %copy-start = (bf16[16,8,128,128]{3,2,1,0:T(8,128)(2,1)S(1)}, bf16[16,8,128,128]{3,2,1,0:T(8,128)(2,1)}, u32[]{:S(2)}) copy-start(bf16[16,8,128,128]{3,2,1,0:T(8,128)(2,1)} %print_ref.3) | copy-start | bytes 12582916
  18.4 0.7 %copy-start.3 = (s32[16,128]{1,0:T(8,128)S(1)}, s32[16,128]{1,0:T(8,128)}, u32[]{:S(2)}) copy-start(s32[16,128]{1,0:T(8,128)} %weeks_ref.3) | copy-start | bytes 24580
  19.1 9.0 %copy-start.1 = (bf16[16,8,128,128]{3,2,1,0:T(8,128)(2,1)S(1)}, bf16[16,8,128,128]{3,2,1,0:T(8,128)(2,1)}, u32[]{:S(2)}) copy-start(bf16[16,8,128,128]{3,2,1,0:T(8,128)(2,1)} %print_ref.3) | copy-start | bytes 12582916
  22.4 5.6 %collective-permute-start.5 = (f32[16,16,128]{2,1,0:T(8,128)S(1)}, f32[16,16,128]{2,1,0:T(8,128)S(1)}, u32[]{:S(2)}, u32[]{:S(2)}) collective-permute-start(f32[16,16,128]{2,1,0:T(8,128)S(1)} %forward.1.own_ref), channel_id=1, source_target_pairs={{0,1},{1,0},{2,3},{3,2},{4,5},{5,4},{6,7},{7,6},{8,9},{9,8},{10,11... | collective-permute-start | bytes 393224 | tf_op jit(solution)/shard_map/ppermute | solution.py:42
  32.9 1.5 %collective-permute-start.6 = (f32[8,64,128]{2,1,0:T(8,128)S(1)}, f32[8,64,128]{2,1,0:T(8,128)S(1)}, u32[]{:S(2)}, u32[]{:S(2)}) collective-permute-start(f32[8,64,128]{2,1,0:T(8,128)S(1)} %get-tuple-element.6), channel_id=1, source_target_pairs={{0,2},{2,0},{4,6},{6,4},{8,10},{10,8},{12,14},{14,12},{16,18},{18,... | collective-permute-start | bytes 786440 | tf_op jit(solution)/shard_map/ppermute | solution.py:42
  34.5 4.7 %collective-permute-start.7 = (f32[2,64,128]{2,1,0:T(8,128)S(1)}, f32[2,64,128]{2,1,0:T(8,128)S(1)}, u32[]{:S(2)}, u32[]{:S(2)}) collective-permute-start(f32[2,64,128]{2,1,0:T(8,128)S(1)} %get-tuple-element.8), channel_id=1, source_target_pairs={{0,8},{2,10},{4,12},{6,14},{8,0},{10,2},{12,4},{14,6},{16,24},{18,... | collective-permute-start | bytes 196616 | tf_op jit(solution)/shard_map/ppermute | solution.py:42
  34.8 6.3 %collective-permute-start.9 = (f32[2,64,128]{2,1,0:T(8,128)S(1)}, f32[2,64,128]{2,1,0:T(8,128)S(1)}, u32[]{:S(2)}, u32[]{:S(2)}) collective-permute-start(f32[2,64,128]{2,1,0:T(8,128)S(1)} %get-tuple-element.9), channel_id=1, source_target_pairs={{0,12},{2,14},{4,8},{6,10},{8,4},{10,6},{12,0},{14,2},{16,28},{18,... | collective-permute-start | bytes 196616 | tf_op jit(solution)/shard_map/ppermute | solution.py:42
  37.5 4.5 %collective-permute-start.8 = (f32[2,64,128]{2,1,0:T(8,128)S(1)}, f32[2,64,128]{2,1,0:T(8,128)S(1)}, u32[]{:S(2)}, u32[]{:S(2)}) collective-permute-start(f32[2,64,128]{2,1,0:T(8,128)S(1)} %get-tuple-element.10), channel_id=1, source_target_pairs={{0,4},{2,6},{4,0},{6,2},{8,12},{10,14},{12,8},{14,10},{16,20},{18,... | collective-permute-start | bytes 196616 | tf_op jit(solution)/shard_map/ppermute | solution.py:42
  42.1 5.2 %collective-permute-start.10 = (f32[1,64,128]{2,1,0:T(8,128)S(1)}, f32[1,64,128]{2,1,0:T(8,128)S(1)}, u32[]{:S(2)}, u32[]{:S(2)}) collective-permute-start(f32[1,64,128]{2,1,0:T(8,128)S(1)} %split.29), channel_id=1, source_target_pairs={{0,16},{2,18},{4,20},{6,22},{8,24},{10,26},{12,28},{14,30},{16,0},... | collective-permute-start | bytes 98312 | tf_op jit(solution)/shard_map/ppermute | solution.py:42

commit v2 on v1

v2 whole, which is shorter than its diff:
```python
import functools

import jax
import jax.numpy as jnp
from jax import lax
from jax.experimental import pallas as pl
from jax.experimental.pallas import tpu as pltpu
from jax.sharding import PartitionSpec as P

MEMBERS = 16
WEEKS = 4
ROWS = WEEKS * MEMBERS

VMEM = pl.BlockSpec(memory_space=pltpu.VMEM)
SMEM = pl.BlockSpec(memory_space=pltpu.SMEM)
HBM = pl.BlockSpec(memory_space=pltpu.HBM)


def phases_of(count):
    bits = [1 << i for i in range(count.bit_length() - 1)]
    upper = bits[:0:-1]
    head = len(upper) % 2
    rounds = [upper[:1]] if head else []
    rounds += [upper[i : i + 2] for i in range(head, len(upper), 2)]
    return [sorted((m | 1 for m in masks_of(bits_of)[1:]), reverse=True) for bits_of in rounds]


def masks_of(bits):
    masks = [0]
    for bit in bits:
        masks += [mask | bit for mask in masks]
    return masks


def order_of(rounds):
    order = [0]
    for masks in rounds:
        order = [mask ^ low for mask in [0] + masks for low in order]
    return order


def swap(value, axis, count, mask):
    return lax.ppermute(value, axis, [(i, i ^ mask) for i in range(count)])


def prepare_kernel(
    rounds,
    gate_ref,
    count_ref,
    blocks_hbm,
    ids_hbm,
    weeks_hbm,
    seen_hbm,
    noise_hbm,
    weight_hbm,
    print_hbm,
    place_ref,
    weeks_ref,
    shift_ref,
    scale_ref,
    held_ref,
    blocks_ref,
    ids_ref,
    seen_ref,
    noise_ref,
    weight_ref,
    sems,
):
    pairs = (
        (blocks_hbm, blocks_ref),
        (ids_hbm, ids_ref),
        (noise_hbm, noise_ref),
        (seen_hbm, seen_ref),
        (weight_hbm, weight_ref),
        (weeks_hbm, weeks_ref),
        (print_hbm, held_ref),
    )
    copies = [pltpu.make_async_copy(src, dst, sems.at[i]) for i, (src, dst) in enumerate(pairs)]
    for copy in copies:
        copy.start()
    for copy in copies[:-1]:
        copy.wait()
    order = order_of(rounds)
    diff = blocks_ref[...] ^ lax.axis_index("obs")
    odd = diff & 1
    place = jnp.zeros_like(diff)
    for masks in rounds:
        low = diff & (functools.reduce(lambda a, b: a | b, masks) & ~1)
        for mask in masks:
            place = place + jnp.where(low == mask & ~1, order.index(mask), 0)
        odd = odd ^ jnp.where(low != 0, 1, 0)
    place_ref[...] = place + odd * len(order)
    column = lax.broadcasted_iota(jnp.int32, (MEMBERS, MEMBERS), 1)
    row = lax.broadcasted_iota(jnp.int32, (MEMBERS, MEMBERS), 0)
    chosen = jnp.zeros((MEMBERS, MEMBERS), jnp.int32)
    for m in range(MEMBERS):
        chosen = jnp.where(row == m, ids_ref[0, m], chosen)
    hot = (column == chosen).astype(jnp.float32).astype(jnp.bfloat16)
    for tile in range(shift_ref.shape[0]):
        shifted = jnp.dot(hot, noise_ref[tile], preferred_element_type=jnp.float32)
        shift_ref[tile] = seen_ref[pl.ds(tile, 1), :] + shifted
    alive = lax.broadcasted_iota(jnp.int32, weight_ref.shape, 0) < count_ref[0]
    scale_ref[...] = jnp.where(alive, jnp.float32(1), jnp.float32(0)) * weight_ref[...]
    copies[-1].wait()


def forward_kernel(place_ref, weeks_ref, mine_ref, other_ref, print_ref, out_ref, flux_ref):
    half = mine_ref.shape[0]
    flux_ref[:half] = mine_ref[...]
    flux_ref[half:] = other_ref[...]
    slots, per_tile = print_ref.shape[:2]
    for tile in range(slots):
        rows = jnp.concatenate([flux_ref[place_ref[j, tile]] for j in range(per_tile)], axis=1)
        sens = jnp.concatenate([print_ref[tile, j] for j in range(per_tile)], axis=1)
        total = lax.dot_general(
            rows, sens, (((1,), (1,)), ((), ())), preferred_element_type=jnp.float32
        )
        weeks = weeks_ref[pl.ds(tile, 1), :]
        picked = total[:MEMBERS]
        for week in range(1, WEEKS):
            picked = jnp.where(weeks == week, total[week * MEMBERS : (week + 1) * MEMBERS], picked)
        out_ref[tile] = picked


def adjoint_kernel(
    place_ref,
    weeks_ref,
    own_ref,
    far_ref,
    shift_ref,
    scale_ref,
    print_ref,
    keep_ref,
    send_ref,
    residual_ref,
    first_ref,
    second_ref,
):
    slots, per_tile = print_ref.shape[:2]
    sums = (first_ref, second_ref)
    for total_ref in sums:
        total_ref[...] = jnp.zeros_like(total_ref)
    for tile in range(slots):
        modeled = own_ref[tile] + far_ref[tile]
        residual = scale_ref[pl.ds(tile, 1), :] * (modeled - shift_ref[tile])
        residual_ref[tile] = residual
        weeks = weeks_ref[pl.ds(tile, 1), :]
        rows = jnp.concatenate(
            [jnp.where(weeks == week, residual, 0.0) for week in range(WEEKS)], axis=0
        ).astype(jnp.bfloat16)
        sens = jnp.concatenate([print_ref[tile, j] for j in range(per_tile)], axis=1)
        part = jnp.dot(rows, sens, preferred_element_type=jnp.float32)
        cells = part.shape[1] // per_tile
        for j in range(per_tile):
            sums[j % 2][place_ref[j, tile]] += part[:, j * cells : (j + 1) * cells]
    half = keep_ref.shape[0]
    keep_ref[...] = first_ref[:half] + second_ref[:half]
    send_ref[...] = first_ref[half:] + second_ref[half:]


def on_device(
    devices,
    slabs,
    flux_field,
    footprint,
    block_index,
    tile_count,
    sounding_week,
    member_ids,
    observed,
    perturb,
    obs_weight,
):
    rounds = phases_of(devices)
    slots, per_tile, sounds, cells = footprint.shape
    half = devices // 2
    params = pltpu.CompilerParams(vmem_limit_bytes=24 << 20)

    def shape(dims, kind):
        return jax.ShapeDtypeStruct(dims, kind)

    have = flux_field[0]
    for masks in rounds:
        gate = have
        got = [swap(have, "obs", devices, m) for m in masks[::-1]][::-1]
        if masks is rounds[-1]:
            break
        wide = lax.optimization_barrier(jnp.concatenate([have] * (len(masks) + 1), axis=0))
        for k, part in enumerate(got):
            wide = lax.dynamic_update_slice(wide, part, ((k + 1) * part.shape[0], 0, 0))
        have = wide
    parts = [have] + got
    small = (
        (block_index.T, pltpu.VMEM),
        (member_ids[None], pltpu.SMEM),
        (sounding_week, None),
        (observed, pltpu.VMEM),
        (perturb, pltpu.VMEM),
        (obs_weight, pltpu.VMEM),
    )
    place, weeks, shift, scale, held = pl.pallas_call(
        functools.partial(prepare_kernel, rounds),
        out_shape=(
            shape((per_tile, slots), jnp.int32),
            shape(sounding_week.shape, jnp.int32),
            shape((slots, MEMBERS, sounds), jnp.float32),
            shape((slots, sounds), jnp.float32),
            shape(footprint.shape, footprint.dtype),
        ),
        in_specs=[VMEM, SMEM] + [HBM] * 7,
        out_specs=(VMEM,) * 5,
        scratch_shapes=[kind(x.shape, x.dtype) for x, kind in small if kind]
        + [pltpu.SemaphoreType.DMA((7,))],
        compiler_params=params,
        cost_estimate=pl.CostEstimate(flops=0, bytes_accessed=2 * footprint.size * 2, transcendentals=0),
        name="prepare",
    )(
        gate,
        tile_count,
        *[pltpu.with_memory_space_constraint(x, pltpu.HBM) for x, _ in small],
        pltpu.with_memory_space_constraint(footprint, pltpu.HBM),
    )
    parts, shift = lax.optimization_barrier((parts, shift))
    have = jnp.concatenate(parts, axis=0)
    other = swap(have, "obs", devices, 1)
    modeled = pl.pallas_call(
        forward_kernel,
        out_shape=shape((slots, MEMBERS, sounds), jnp.float32),
        in_specs=[SMEM, VMEM, VMEM, VMEM, VMEM],
        out_specs=VMEM,
        scratch_shapes=[pltpu.VMEM((devices, ROWS, cells), jnp.bfloat16)],
        compiler_params=params,
        name="forward",
    )(place, weeks, have, other, held)
    mask = 1
    while 2 * mask < slabs:
        modeled = modeled + swap(modeled, "cell", slabs, mask)
        mask *= 2
    far = swap(modeled, "cell", slabs, mask)
    keep, send, residual = pl.pallas_call(
        adjoint_kernel,
        out_shape=(
            shape((half, ROWS, cells), jnp.float32),
            shape((half, ROWS, cells), jnp.float32),
            shape((slots, MEMBERS, sounds), jnp.float32),
        ),
        in_specs=[SMEM] + [VMEM] * 6,
        out_specs=(VMEM, VMEM, VMEM),
        scratch_shapes=[pltpu.VMEM((devices, ROWS, cells), jnp.float32)] * 2,
        compiler_params=params,
        name="adjoint",
    )(place, weeks, modeled, far, shift, scale, held)
    total = keep + swap(send, "obs", devices, 1)
    for masks in rounds[::-1]:
        pieces = jnp.split(total, len(masks) + 1, axis=0)
        total = pieces[0]
        for mask, piece in zip(masks, pieces[1:]):
            total = total + swap(piece, "obs", devices, mask)
    return (total[None], residual.astype(jnp.bfloat16))


def solution(mesh):
    devices, slabs = mesh.shape["obs"], mesh.shape["cell"]
    return jax.shard_map(
        functools.partial(on_device, devices, slabs),
        mesh=mesh,
        in_specs=(
            P("cell", "obs", None, None),
            P("obs", "cell", None, None),
            P("obs", "cell"),
            P("obs"),
            P("obs", None),
            P(),
            P("obs", None),
            P("obs", None, None),
            P("obs", None),
        ),
        out_specs=(P("cell", "obs", None, None), P("obs", None, None)),
        check_vma=False,
    )
```

time: 48.4 us -> 39.2 us (0.81)
  local copies, waits for them, and re-layouts: 4.48 us -> 0.06 us
  waiting for transfers between devices: 17 us -> 14.3 us
  Pallas kernels: 8.16 us -> 6.29 us
  starting transfers between devices: 15.5 us -> 14.7 us
  other arithmetic: 1.39 us -> 2.09 us
    unnamed x19 -> x3, local copies, waits for them, and re-layouts: 4.45 us -> 0.02 us
    ppermute x11, waiting for transfers between devices: 17 us -> 14.3 us  [swap(): return lax.ppermute(value, axis, [(i, i ^ mask) for i in range(count)])]
    pallas_call x2 -> x3, Pallas kernels: 8.16 us -> 6.29 us  [the longest x1 2.36 us: on_device(): pl.pallas_call(functools.partial(prepare_kernel, rounds), out_shape=(shap...]
    ppermute x11, starting transfers between devices: 15.5 us -> 14.7 us  [swap(): return lax.ppermute(value, axis, [(i, i ^ mask) for i in range(count)])]
    convert_element_type x0 -> x1, other arithmetic: none -> 0.64 us  [on_device(): return (total[None], residual.astype(jnp.bfloat16))]
  transfers between devices with their start and end apart: 11 -> 11, of which waited for: 9 -> 8; matrix products, arithmetic and copies ran while one was open for 3% -> 4% of each run, Pallas kernels for 0% -> 6%
where the time goes in v2:
time: 39.2 us; the launch traced here: 38.8 us
  starting transfers between devices  14.7 us (38%)
  waiting for transfers between devices  14.3 us (36%)
  Pallas kernels  6.29 us (16%)
  other arithmetic  2.09 us (5%)
  between operations  1.37 us (3%)
    ppermute x11, starting transfers between devices, swap(): return lax.ppermute(value, axis, [(i, i ^ mask) for i in range(count)])  14.7 us
    ppermute x11, waiting for transfers between devices, swap(): return lax.ppermute(value, axis, [(i, i ^ mask) for i in range(count)])  14.3 us
    pallas_call x1, Pallas kernels, on_device(): pl.pallas_call(functools.partial(prepare_kernel, rounds), out_shape=(shap...  2.36 us
    pallas_call x1, Pallas kernels, on_device(): pl.pallas_call(forward_kernel, out_shape=shape((slots, MEMBERS, sounds),...  2.15 us
    pallas_call x1, Pallas kernels, on_device(): pl.pallas_call(adjoint_kernel, out_shape=(shape((half, ROWS, cells), jnp....  1.78 us
    concatenate x1, other arithmetic, on_device(): jnp.concatenate([have] * (len(masks) + 1), axis=0)  0.79 us
  transfers between devices with their start and end apart: 11, of which 8 were waited for; matrix products, arithmetic and copies ran while one was open for 4% of the time, Pallas kernels for 6%

profile of v2, /device:TPU:0, one launch (start us, length us, event | category | flops | bytes accessed | tf_op | source)
XLA Modules:
  0.0 38.8 jit_solution(6033219556733309510)
XLA Ops:
  0.6 3.5 %collective-permute-start = (bf16[1,64,128]{2,1,0:T(8,128)(2,1)}, bf16[1,64,128]{2,1,0:T(8,128)(2,1)S(1)}, u32[]{:S(2)}, u32[]{:S(2)}) collective-permute-start(bf16[1,64,128]{2,1,0:T(8,128)(2,1)} %bitcast.5), channel_id=1, source_target_pairs={{0,18},{2,16},{4,22},{6,20},{8,26},{10,24},{12,30},{14,28},{16,2},... | collective-permute-start | bytes 49160 | tf_op jit(solution)/shard_map/ppermute | solution.py:43
  4.2 0.8 %pad_maximum_fusion = bf16[2,64,128]{2,1,0:T(8,128)(2,1)S(1)} fusion(bf16[1,64,128]{2,1,0:T(8,128)(2,1)} %bitcast.6), kind=kLoop, calls=%fused_computation.5 | loop fusion | flops 16384 | bytes 49152 | tf_op jit(solution)/shard_map/concatenate | solution.py:188
  5.0 0.9 %collective-permute-done = bf16[1,64,128]{2,1,0:T(8,128)(2,1)S(1)} collective-permute-done((bf16[1,64,128]{2,1,0:T(8,128)(2,1)}, bf16[1,64,128]{2,1,0:T(8,128)(2,1)S(1)}, u32[]{:S(2)}, u32[]{:S(2)}) %collective-permute-start) | collective-permute-done | bytes 16416 | tf_op jit(solution)/shard_map/ppermute | solution.py:43
  5.8 1.8 %collective-permute-start.3 = (bf16[2,64,128]{2,1,0:T(8,128)(2,1)S(1)}, bf16[2,64,128]{2,1,0:T(8,128)(2,1)S(1)}, u32[]{:S(2)}, u32[]{:S(2)}) collective-permute-start(bf16[2,64,128]{2,1,0:T(8,128)(2,1)S(1)} %constant_dynamic-update-slice_fusion.4.gate_ref), channel_id=1, source_target_pairs={{0,6},{2,4},{4,2},{6,0},{8,14},{10,12},{12,10},{14,8},{16,22},{18,... | collective-permute-start | bytes 98312 | tf_op jit(solution)/shard_map/ppermute | solution.py:43
  7.6 1.6 %collective-permute-start.2 = (bf16[2,64,128]{2,1,0:T(8,128)(2,1)S(1)}, bf16[2,64,128]{2,1,0:T(8,128)(2,1)S(1)}, u32[]{:S(2)}, u32[]{:S(2)}) collective-permute-start(bf16[2,64,128]{2,1,0:T(8,128)(2,1)S(1)} %constant_dynamic-update-slice_fusion.4.gate_ref), channel_id=1, source_target_pairs={{0,10},{2,8},{4,14},{6,12},{8,2},{10,0},{12,6},{14,4},{16,26},{18,... | collective-permute-start | bytes 98312 | tf_op jit(solution)/shard_map/ppermute | solution.py:43
  9.2 0.1 collective-permute-start.1
  10.0 2.4 %prepare.1 = (s32[8,16]{1,0:T(8,128)S(1)}, s32[16,128]{1,0:T(8,128)S(1)}, f32[16,16,128]{2,1,0:T(8,128)S(1)}, f32[16,128]{1,0:T(8,128)S(1)}, bf16[16,8,128,128]{3,2,1,0:T(8,128)(2,1)S(1)}) custom-call(bf16[2,64,128]{2,1,0:T(8,128)(2,1)S(1)} %constant_dynamic-update-slice_fusion.4.gate_ref, s32[1]{0:T(128)S(6)} %copy.15.count_ref, s32[8,16]{1,0:T(8,128)} %bitcast.7, ...), custom_call_target="tpu_custom_call" | custom-call | bytes 8388608 | tf_op jit(solution)/shard_map/prepare/pallas_call | solution.py:201
  12.3 0.0 collective-permute-done.3
  12.3 0.0 collective-permute-done.2
  12.3 1.2 %collective-permute-done.1 = bf16[2,64,128]{2,1,0:T(8,128)(2,1)S(1)} collective-permute-done((bf16[2,64,128]{2,1,0:T(8,128)(2,1)S(1)}, bf16[2,64,128]{2,1,0:T(8,128)(2,1)S(1)}, u32[]{:S(2)}, u32[]{:S(2)}) %collective-permute-start.1) | collective-permute-done | bytes 32800 | tf_op jit(solution)/shard_map/ppermute | solution.py:43
  13.6 0.2 collective-permute-start.4
  13.8 1.2 %collective-permute-done.4.other_ref = bf16[8,64,128]{2,1,0:T(8,128)(2,1)S(1)} collective-permute-done((bf16[8,64,128]{2,1,0:T(8,128)(2,1)S(1)}, bf16[8,64,128]{2,1,0:T(8,128)(2,1)S(1)}, u32[]{:S(2)}, u32[]{:S(2)}) %collective-permute-start.4) | collective-permute-done | bytes 131104 | tf_op jit(solution)/shard_map/ppermute | solution.py:43
  15.0 2.1 %forward.1.own_ref = f32[16,16,128]{2,1,0:T(8,128)S(1)} custom-call(s32[8,16]{1,0:T(8,128)S(1)} %get-tuple-element.15.place_ref, s32[16,128]{1,0:T(8,128)S(1)} %get-tuple-element.16.weeks_ref, bf16[8,64,128]{2,1,0:T(8,128)(2,1)S(1)} %constant_dynamic-update-slice_fusion.mine_ref, bf16[8,64,128]{2,1,0:T(8,128)(2,1)S(1)} %collective-permute-done.4.other_ref, ...), custom_call_target="tpu_custom_call" | custom-call | tf_op jit(solution)/shard_map/forward/pallas_call | solution.py:226
  17.2 1.6 %collective-permute-start.5 = (f32[16,16,128]{2,1,0:T(8,128)S(1)}, f32[16,16,128]{2,1,0:T(8,128)S(1)}, u32[]{:S(2)}, u32[]{:S(2)}) collective-permute-start(f32[16,16,128]{2,1,0:T(8,128)S(1)} %forward.1.own_ref), channel_id=1, source_target_pairs={{0,1},{1,0},{2,3},{3,2},{4,5},{5,4},{6,7},{7,6},{8,9},{9,8},{10,11... | collective-permute-start | bytes 393224 | tf_op jit(solution)/shard_map/ppermute | solution.py:43
  18.8 4.0 %collective-permute-done.5.far_ref = f32[16,16,128]{2,1,0:T(8,128)S(1)} collective-permute-done((f32[16,16,128]{2,1,0:T(8,128)S(1)}, f32[16,16,128]{2,1,0:T(8,128)S(1)}, u32[]{:S(2)}, u32[]{:S(2)}) %collective-permute-start.5) | collective-permute-done | bytes 131104 | tf_op jit(solution)/shard_map/ppermute | solution.py:43
  22.8 1.8 %adjoint.1 = (f32[8,64,128]{2,1,0:T(8,128)S(1)}, f32[8,64,128]{2,1,0:T(8,128)S(1)}, f32[16,16,128]{2,1,0:T(8,128)S(1)}) custom-call(s32[8,16]{1,0:T(8,128)S(1)} %get-tuple-element.15.place_ref, s32[16,128]{1,0:T(8,128)S(1)} %get-tuple-element.16.weeks_ref, f32[16,16,128]{2,1,0:T(8,128)S(1)} %forward.1.own_ref, ...), custom_call_target="tpu_custom_call" | custom-call | tf_op jit(solution)/shard_map/adjoint/pallas_call | solution.py:240
  24.6 0.1 collective-permute-start.6
  24.7 1.5 %collective-permute-done.6 = f32[8,64,128]{2,1,0:T(8,128)S(1)} collective-permute-done((f32[8,64,128]{2,1,0:T(8,128)S(1)}, f32[8,64,128]{2,1,0:T(8,128)S(1)}, u32[]{:S(2)}, u32[]{:S(2)}) %collective-permute-start.6) | collective-permute-done | bytes 262176 | tf_op jit(solution)/shard_map/ppermute | solution.py:43
  26.3 1.4 %collective-permute-start.7 = (f32[2,64,128]{2,1,0:T(8,128)S(1)}, f32[2,64,128]{2,1,0:T(8,128)S(1)}, u32[]{:S(2)}, u32[]{:S(2)}) collective-permute-start(f32[2,64,128]{2,1,0:T(8,128)S(1)} %get-tuple-element.28), channel_id=1, source_target_pairs={{0,14},{2,12},{4,10},{6,8},{8,6},{10,4},{12,2},{14,0},{16,30},{18,... | collective-permute-start | bytes 196616 | tf_op jit(solution)/shard_map/ppermute | solution.py:43
  27.7 0.5 %collective-permute-start.9 = (f32[2,64,128]{2,1,0:T(8,128)S(1)}, f32[2,64,128]{2,1,0:T(8,128)S(1)}, u32[]{:S(2)}, u32[]{:S(2)}) collective-permute-start(f32[2,64,128]{2,1,0:T(8,128)S(1)} %get-tuple-element.29), channel_id=1, source_target_pairs={{0,6},{2,4},{4,2},{6,0},{8,14},{10,12},{12,10},{14,8},{16,22},{18,... | collective-permute-start | bytes 196616 | tf_op jit(solution)/shard_map/ppermute | solution.py:43
  28.2 1.1 %collective-permute-start.8 = (f32[2,64,128]{2,1,0:T(8,128)S(1)}, f32[2,64,128]{2,1,0:T(8,128)S(1)}, u32[]{:S(2)}, u32[]{:S(2)}) collective-permute-start(f32[2,64,128]{2,1,0:T(8,128)S(1)} %get-tuple-element.30), channel_id=1, source_target_pairs={{0,10},{2,8},{4,14},{6,12},{8,2},{10,0},{12,6},{14,4},{16,26},{18,... | collective-permute-start | bytes 196616 | tf_op jit(solution)/shard_map/ppermute | solution.py:43
  29.3 2.1 %collective-permute-done.7 = f32[2,64,128]{2,1,0:T(8,128)S(1)} collective-permute-done((f32[2,64,128]{2,1,0:T(8,128)S(1)}, f32[2,64,128]{2,1,0:T(8,128)S(1)}, u32[]{:S(2)}, u32[]{:S(2)}) %collective-permute-start.7) | collective-permute-done | bytes 65568 | tf_op jit(solution)/shard_map/ppermute | solution.py:43
  31.4 1.6 %collective-permute-done.9 = f32[2,64,128]{2,1,0:T(8,128)S(1)} collective-permute-done((f32[2,64,128]{2,1,0:T(8,128)S(1)}, f32[2,64,128]{2,1,0:T(8,128)S(1)}, u32[]{:S(2)}, u32[]{:S(2)}) %collective-permute-start.9) | collective-permute-done | bytes 65568 | tf_op jit(solution)/shard_map/ppermute | solution.py:43
  33.0 0.0 collective-permute-done.8
  33.0 2.8 %collective-permute-start.10 = (f32[1,64,128]{2,1,0:T(8,128)S(1)}, f32[1,64,128]{2,1,0:T(8,128)S(1)}, u32[]{:S(2)}, u32[]{:S(2)}) collective-permute-start(f32[1,64,128]{2,1,0:T(8,128)S(1)} %split.29), channel_id=1, source_target_pairs={{0,18},{2,16},{4,22},{6,20},{8,26},{10,24},{12,30},{14,28},{16,2},... | collective-permute-start | bytes 98312 | tf_op jit(solution)/shard_map/ppermute | solution.py:43
  35.8 0.6 %convert_element_type.3 = bf16[16,16,128]{2,1,0:T(8,128)(2,1)} convert(f32[16,16,128]{2,1,0:T(8,128)S(1)} %get-tuple-element.27) | non-fusion elementwise | flops 32768 | bytes 196608 | tf_op jit(solution)/shard_map/convert_element_type | solution.py:259
  36.4 1.8 %collective-permute-done.10 = f32[1,64,128]{2,1,0:T(8,128)S(1)} collective-permute-done((f32[1,64,128]{2,1,0:T(8,128)S(1)}, f32[1,64,128]{2,1,0:T(8,128)S(1)}, u32[]{:S(2)}, u32[]{:S(2)}) %collective-permute-start.10) | collective-permute-done | bytes 32800 | tf_op jit(solution)/shard_map/ppermute | solution.py:43
  38.2 0.6 %fusion.2 = f32[1,1,64,128]{3,2,1,0:T(8,128)} fusion(f32[1,64,128]{2,1,0:T(8,128)S(1)} %collective-permute-done.10, f32[2,64,128]{2,1,0:T(8,128)S(1)} %fusion.1), kind=kLoop, calls=%fused_computation.4 | loop fusion | flops 8192 | bytes 98304 | tf_op jit(solution)/shard_map/broadcast_in_dim | solution.py:259
  (9 shorter events, 0.1 us)
Async XLA Ops:
  0.6 5.2 %collective-permute-start = (bf16[1,64,128]{2,1,0:T(8,128)(2,1)}, bf16[1,64,128]{2,1,0:T(8,128)(2,1)S(1)}, u32[]{:S(2)}, u32[]{:S(2)}) collective-permute-start(bf16[1,64,128]{2,1,0:T(8,128)(2,1)} %bitcast.5), channel_id=1, source_target_pairs={{0,18},{2,16},{4,22},{6,20},{8,26},{10,24},{12,30},{14,28},{16,2},... | collective-permute-start | bytes 49160 | tf_op jit(solution)/shard_map/ppermute | solution.py:43
  5.8 6.5 %collective-permute-start.3 = (bf16[2,64,128]{2,1,0:T(8,128)(2,1)S(1)}, bf16[2,64,128]{2,1,0:T(8,128)(2,1)S(1)}, u32[]{:S(2)}, u32[]{:S(2)}) collective-permute-start(bf16[2,64,128]{2,1,0:T(8,128)(2,1)S(1)} %constant_dynamic-update-slice_fusion.4.gate_ref), channel_id=1, source_target_pairs={{0,6},{2,4},{4,2},{6,0},{8,14},{10,12},{12,10},{14,8},{16,22},{18,... | collective-permute-start | bytes 98312 | tf_op jit(solution)/shard_map/ppermute | solution.py:43
  7.6 4.7 %collective-permute-start.2 = (bf16[2,64,128]{2,1,0:T(8,128)(2,1)S(1)}, bf16[2,64,128]{2,1,0:T(8,128)(2,1)S(1)}, u32[]{:S(2)}, u32[]{:S(2)}) collective-permute-start(bf16[2,64,128]{2,1,0:T(8,128)(2,1)S(1)} %constant_dynamic-update-slice_fusion.4.gate_ref), channel_id=1, source_target_pairs={{0,10},{2,8},{4,14},{6,12},{8,2},{10,0},{12,6},{14,4},{16,26},{18,... | collective-permute-start | bytes 98312 | tf_op jit(solution)/shard_map/ppermute | solution.py:43
  9.2 4.3 %collective-permute-start.1 = (bf16[2,64,128]{2,1,0:T(8,128)(2,1)S(1)}, bf16[2,64,128]{2,1,0:T(8,128)(2,1)S(1)}, u32[]{:S(2)}, u32[]{:S(2)}) collective-permute-start(bf16[2,64,128]{2,1,0:T(8,128)(2,1)S(1)} %constant_dynamic-update-slice_fusion.4.gate_ref), channel_id=1, source_target_pairs={{0,14},{2,12},{4,10},{6,8},{8,6},{10,4},{12,2},{14,0},{16,30},{18,... | collective-permute-start | bytes 98312 | tf_op jit(solution)/shard_map/ppermute | solution.py:43
  13.6 1.4 %collective-permute-start.4 = (bf16[8,64,128]{2,1,0:T(8,128)(2,1)S(1)}, bf16[8,64,128]{2,1,0:T(8,128)(2,1)S(1)}, u32[]{:S(2)}, u32[]{:S(2)}) collective-permute-start(bf16[8,64,128]{2,1,0:T(8,128)(2,1)S(1)} %constant_dynamic-update-slice_fusion.mine_ref), channel_id=1, source_target_pairs={{0,2},{2,0},{4,6},{6,4},{8,10},{10,8},{12,14},{14,12},{16,18},{18,... | collective-permute-start | bytes 393224 | tf_op jit(solution)/shard_map/ppermute | solution.py:43
  17.2 5.6 %collective-permute-start.5 = (f32[16,16,128]{2,1,0:T(8,128)S(1)}, f32[16,16,128]{2,1,0:T(8,128)S(1)}, u32[]{:S(2)}, u32[]{:S(2)}) collective-permute-start(f32[16,16,128]{2,1,0:T(8,128)S(1)} %forward.1.own_ref), channel_id=1, source_target_pairs={{0,1},{1,0},{2,3},{3,2},{4,5},{5,4},{6,7},{7,6},{8,9},{9,8},{10,11... | collective-permute-start | bytes 393224 | tf_op jit(solution)/shard_map/ppermute | solution.py:43
  24.6 1.6 %collective-permute-start.6 = (f32[8,64,128]{2,1,0:T(8,128)S(1)}, f32[8,64,128]{2,1,0:T(8,128)S(1)}, u32[]{:S(2)}, u32[]{:S(2)}) collective-permute-start(f32[8,64,128]{2,1,0:T(8,128)S(1)} %get-tuple-element.26), channel_id=1, source_target_pairs={{0,2},{2,0},{4,6},{6,4},{8,10},{10,8},{12,14},{14,12},{16,18},{18,... | collective-permute-start | bytes 786440 | tf_op jit(solution)/shard_map/ppermute | solution.py:43
  26.3 5.1 %collective-permute-start.7 = (f32[2,64,128]{2,1,0:T(8,128)S(1)}, f32[2,64,128]{2,1,0:T(8,128)S(1)}, u32[]{:S(2)}, u32[]{:S(2)}) collective-permute-start(f32[2,64,128]{2,1,0:T(8,128)S(1)} %get-tuple-element.28), channel_id=1, source_target_pairs={{0,14},{2,12},{4,10},{6,8},{8,6},{10,4},{12,2},{14,0},{16,30},{18,... | collective-permute-start | bytes 196616 | tf_op jit(solution)/shard_map/ppermute | solution.py:43
  27.7 5.3 %collective-permute-start.9 = (f32[2,64,128]{2,1,0:T(8,128)S(1)}, f32[2,64,128]{2,1,0:T(8,128)S(1)}, u32[]{:S(2)}, u32[]{:S(2)}) collective-permute-start(f32[2,64,128]{2,1,0:T(8,128)S(1)} %get-tuple-element.29), channel_id=1, source_target_pairs={{0,6},{2,4},{4,2},{6,0},{8,14},{10,12},{12,10},{14,8},{16,22},{18,... | collective-permute-start | bytes 196616 | tf_op jit(solution)/shard_map/ppermute | solution.py:43
  28.2 4.8 %collective-permute-start.8 = (f32[2,64,128]{2,1,0:T(8,128)S(1)}, f32[2,64,128]{2,1,0:T(8,128)S(1)}, u32[]{:S(2)}, u32[]{:S(2)}) collective-permute-start(f32[2,64,128]{2,1,0:T(8,128)S(1)} %get-tuple-element.30), channel_id=1, source_target_pairs={{0,10},{2,8},{4,14},{6,12},{8,2},{10,0},{12,6},{14,4},{16,26},{18,... | collective-permute-start | bytes 196616 | tf_op jit(solution)/shard_map/ppermute | solution.py:43
  33.0 5.2 %collective-permute-start.10 = (f32[1,64,128]{2,1,0:T(8,128)S(1)}, f32[1,64,128]{2,1,0:T(8,128)S(1)}, u32[]{:S(2)}, u32[]{:S(2)}) collective-permute-start(f32[1,64,128]{2,1,0:T(8,128)S(1)} %split.29), channel_id=1, source_target_pairs={{0,18},{2,16},{4,22},{6,20},{8,26},{10,24},{12,30},{14,28},{16,2},... | collective-permute-start | bytes 98312 | tf_op jit(solution)/shard_map/ppermute | solution.py:43

commit v3 on v2

--- a/solution.py
+++ b/solution.py
@@ -125,8 +125,7 @@
 def adjoint_kernel(
     place_ref,
     weeks_ref,
-    own_ref,
-    far_ref,
+    modeled_ref,
     shift_ref,
     scale_ref,
     print_ref,
@@ -141,8 +140,7 @@
     for total_ref in sums:
         total_ref[...] = jnp.zeros_like(total_ref)
     for tile in range(slots):
-        modeled = own_ref[tile] + far_ref[tile]
-        residual = scale_ref[pl.ds(tile, 1), :] * (modeled - shift_ref[tile])
+        residual = scale_ref[pl.ds(tile, 1), :] * (modeled_ref[tile] - shift_ref[tile])
         residual_ref[tile] = residual
         weeks = weeks_ref[pl.ds(tile, 1), :]
         rows = jnp.concatenate(
@@ -236,7 +234,9 @@
     while 2 * mask < slabs:
         modeled = modeled + swap(modeled, "cell", slabs, mask)
         mask *= 2
+    modeled = modeled.astype(jnp.float16)
     far = swap(modeled, "cell", slabs, mask)
+    modeled = modeled.astype(jnp.float32) + far.astype(jnp.float32)
     keep, send, residual = pl.pallas_call(
         adjoint_kernel,
         out_shape=(
@@ -244,12 +244,12 @@
             shape((half, ROWS, cells), jnp.float32),
             shape((slots, MEMBERS, sounds), jnp.float32),
         ),
-        in_specs=[SMEM] + [VMEM] * 6,
+        in_specs=[SMEM] + [VMEM] * 5,
         out_specs=(VMEM, VMEM, VMEM),
         scratch_shapes=[pltpu.VMEM((devices, ROWS, cells), jnp.float32)] * 2,
         compiler_params=params,
         name="adjoint",
-    )(place, weeks, modeled, far, shift, scale, held)
+    )(place, weeks, modeled, shift, scale, held)
     total = keep + swap(send, "obs", devices, 1)
     for masks in rounds[::-1]:
         pieces = jnp.split(total, len(masks) + 1, axis=0)

time: 39.2 us -> 37.8 us (0.964)
  waiting for transfers between devices: 14.3 us -> 13.1 us
    ppermute x11, waiting for transfers between devices: 14.3 us -> 13.1 us  [swap(): return lax.ppermute(value, axis, [(i, i ^ mask) for i in range(count)])]
where the time goes in v3:
time: 37.8 us; the launch traced here: 37.4 us
  starting transfers between devices  14.7 us (39%)
  waiting for transfers between devices  13.1 us (35%)
  Pallas kernels  6.15 us (16%)
  other arithmetic  2.12 us (6%)
  between operations  1.38 us (4%)
    ppermute x11, starting transfers between devices, swap(): return lax.ppermute(value, axis, [(i, i ^ mask) for i in range(count)])  14.7 us
    ppermute x11, waiting for transfers between devices, swap(): return lax.ppermute(value, axis, [(i, i ^ mask) for i in range(count)])  13.1 us
    pallas_call x1, Pallas kernels, on_device(): pl.pallas_call(functools.partial(prepare_kernel, rounds), out_shape=(shap...  2.36 us
    pallas_call x1, Pallas kernels, on_device(): pl.pallas_call(forward_kernel, out_shape=shape((slots, MEMBERS, sounds),...  2.15 us
    pallas_call x1, Pallas kernels, on_device(): pl.pallas_call(adjoint_kernel, out_shape=(shape((half, ROWS, cells), jnp....  1.63 us
    concatenate x1, other arithmetic, on_device(): jnp.concatenate([have] * (len(masks) + 1), axis=0)  0.79 us
  transfers between devices with their start and end apart: 11, of which 8 were waited for; matrix products, arithmetic and copies ran while one was open for 4% of the time, Pallas kernels for 6%

profile of v3, /device:TPU:0, one launch (start us, length us, event | category | flops | bytes accessed | tf_op | source)
XLA Modules:
  0.0 37.4 jit_solution(16330908169437171111)
XLA Ops:
  0.6 3.5 %collective-permute-start = (bf16[1,64,128]{2,1,0:T(8,128)(2,1)}, bf16[1,64,128]{2,1,0:T(8,128)(2,1)S(1)}, u32[]{:S(2)}, u32[]{:S(2)}) collective-permute-start(bf16[1,64,128]{2,1,0:T(8,128)(2,1)} %bitcast.5), channel_id=1, source_target_pairs={{0,18},{2,16},{4,22},{6,20},{8,26},{10,24},{12,30},{14,28},{16,2},... | collective-permute-start | bytes 49160 | tf_op jit(solution)/shard_map/ppermute | solution.py:43
  4.2 0.8 %pad_maximum_fusion = bf16[2,64,128]{2,1,0:T(8,128)(2,1)S(1)} fusion(bf16[1,64,128]{2,1,0:T(8,128)(2,1)} %bitcast.6), kind=kLoop, calls=%fused_computation.6 | loop fusion | flops 16384 | bytes 49152 | tf_op jit(solution)/shard_map/concatenate | solution.py:186
  5.0 0.9 %collective-permute-done = bf16[1,64,128]{2,1,0:T(8,128)(2,1)S(1)} collective-permute-done((bf16[1,64,128]{2,1,0:T(8,128)(2,1)}, bf16[1,64,128]{2,1,0:T(8,128)(2,1)S(1)}, u32[]{:S(2)}, u32[]{:S(2)}) %collective-permute-start) | collective-permute-done | bytes 16416 | tf_op jit(solution)/shard_map/ppermute | solution.py:43
  5.8 1.8 %collective-permute-start.3 = (bf16[2,64,128]{2,1,0:T(8,128)(2,1)S(1)}, bf16[2,64,128]{2,1,0:T(8,128)(2,1)S(1)}, u32[]{:S(2)}, u32[]{:S(2)}) collective-permute-start(bf16[2,64,128]{2,1,0:T(8,128)(2,1)S(1)} %constant_dynamic-update-slice_fusion.4.gate_ref), channel_id=1, source_target_pairs={{0,6},{2,4},{4,2},{6,0},{8,14},{10,12},{12,10},{14,8},{16,22},{18,... | collective-permute-start | bytes 98312 | tf_op jit(solution)/shard_map/ppermute | solution.py:43
  7.6 1.6 %collective-permute-start.2 = (bf16[2,64,128]{2,1,0:T(8,128)(2,1)S(1)}, bf16[2,64,128]{2,1,0:T(8,128)(2,1)S(1)}, u32[]{:S(2)}, u32[]{:S(2)}) collective-permute-start(bf16[2,64,128]{2,1,0:T(8,128)(2,1)S(1)} %constant_dynamic-update-slice_fusion.4.gate_ref), channel_id=1, source_target_pairs={{0,10},{2,8},{4,14},{6,12},{8,2},{10,0},{12,6},{14,4},{16,26},{18,... | collective-permute-start | bytes 98312 | tf_op jit(solution)/shard_map/ppermute | solution.py:43
  9.2 0.1 collective-permute-start.1
  10.0 2.4 %prepare.1 = (s32[8,16]{1,0:T(8,128)S(1)}, s32[16,128]{1,0:T(8,128)S(1)}, f32[16,16,128]{2,1,0:T(8,128)S(1)}, f32[16,128]{1,0:T(8,128)S(1)}, bf16[16,8,128,128]{3,2,1,0:T(8,128)(2,1)S(1)}) custom-call(bf16[2,64,128]{2,1,0:T(8,128)(2,1)S(1)} %constant_dynamic-update-slice_fusion.4.gate_ref, s32[1]{0:T(128)S(6)} %copy.15.count_ref, s32[8,16]{1,0:T(8,128)} %bitcast.7, ...), custom_call_target="tpu_custom_call" | custom-call | bytes 8388608 | tf_op jit(solution)/shard_map/prepare/pallas_call | solution.py:199
  12.3 0.0 collective-permute-done.3
  12.3 0.0 collective-permute-done.2
  12.3 1.2 %collective-permute-done.1 = bf16[2,64,128]{2,1,0:T(8,128)(2,1)S(1)} collective-permute-done((bf16[2,64,128]{2,1,0:T(8,128)(2,1)S(1)}, bf16[2,64,128]{2,1,0:T(8,128)(2,1)S(1)}, u32[]{:S(2)}, u32[]{:S(2)}) %collective-permute-start.1) | collective-permute-done | bytes 32800 | tf_op jit(solution)/shard_map/ppermute | solution.py:43
  13.6 0.2 collective-permute-start.4
  13.8 1.2 %collective-permute-done.4.other_ref = bf16[8,64,128]{2,1,0:T(8,128)(2,1)S(1)} collective-permute-done((bf16[8,64,128]{2,1,0:T(8,128)(2,1)S(1)}, bf16[8,64,128]{2,1,0:T(8,128)(2,1)S(1)}, u32[]{:S(2)}, u32[]{:S(2)}) %collective-permute-start.4) | collective-permute-done | bytes 131104 | tf_op jit(solution)/shard_map/ppermute | solution.py:43
  15.0 2.2 %forward.1 = f32[16,16,128]{2,1,0:T(8,128)S(1)} custom-call(s32[8,16]{1,0:T(8,128)S(1)} %get-tuple-element.15.place_ref, s32[16,128]{1,0:T(8,128)S(1)} %get-tuple-element.16.weeks_ref, bf16[8,64,128]{2,1,0:T(8,128)(2,1)S(1)} %constant_dynamic-update-slice_fusion.mine_ref, bf16[8,64,128]{2,1,0:T(8,128)(2,1)S(1)} %collective-permute-done.4.other_ref, ...), custom_call_target="tpu_custom_call" | custom-call | tf_op jit(solution)/shard_map/forward/pallas_call | solution.py:224
  17.2 1.6 %collective-permute-start.5 = (f16[16,16,128]{2,1,0:T(8,128)(2,1)S(1)}, f16[16,16,128]{2,1,0:T(8,128)(2,1)S(1)}, u32[]{:S(2)}, u32[]{:S(2)}) collective-permute-start(f16[16,16,128]{2,1,0:T(8,128)(2,1)S(1)} %convert_element_type.12), channel_id=1, source_target_pairs={{0,1},{1,0},{2,3},{3,2},{4,5},{5,4},{6,7},{7,6},{8,9},{9,8},{10,11... | collective-permute-start | bytes 196616 | tf_op jit(solution)/shard_map/ppermute | solution.py:43
  18.8 2.7 %collective-permute-done.5 = f16[16,16,128]{2,1,0:T(8,128)(2,1)S(1)} collective-permute-done((f16[16,16,128]{2,1,0:T(8,128)(2,1)S(1)}, f16[16,16,128]{2,1,0:T(8,128)(2,1)S(1)}, u32[]{:S(2)}, u32[]{:S(2)}) %collective-permute-start.5) | collective-permute-done | bytes 65568 | tf_op jit(solution)/shard_map/ppermute | solution.py:43
  21.6 1.6 %adjoint.1 = (f32[8,64,128]{2,1,0:T(8,128)S(1)}, f32[8,64,128]{2,1,0:T(8,128)S(1)}, f32[16,16,128]{2,1,0:T(8,128)S(1)}) custom-call(s32[8,16]{1,0:T(8,128)S(1)} %get-tuple-element.15.place_ref, s32[16,128]{1,0:T(8,128)S(1)} %get-tuple-element.16.weeks_ref, f32[16,16,128]{2,1,0:T(8,128)S(1)} %convert_add_fusion.modeled_ref, ...), custom_call_target="tpu_custom_call" | custom-call | tf_op jit(solution)/shard_map/adjoint/pallas_call | solution.py:240
  23.2 0.1 collective-permute-start.6
  23.3 1.5 %collective-permute-done.6 = f32[8,64,128]{2,1,0:T(8,128)S(1)} collective-permute-done((f32[8,64,128]{2,1,0:T(8,128)S(1)}, f32[8,64,128]{2,1,0:T(8,128)S(1)}, u32[]{:S(2)}, u32[]{:S(2)}) %collective-permute-start.6) | collective-permute-done | bytes 262176 | tf_op jit(solution)/shard_map/ppermute | solution.py:43
  24.9 1.3 %collective-permute-start.7 = (f32[2,64,128]{2,1,0:T(8,128)S(1)}, f32[2,64,128]{2,1,0:T(8,128)S(1)}, u32[]{:S(2)}, u32[]{:S(2)}) collective-permute-start(f32[2,64,128]{2,1,0:T(8,128)S(1)} %get-tuple-element.28), channel_id=1, source_target_pairs={{0,14},{2,12},{4,10},{6,8},{8,6},{10,4},{12,2},{14,0},{16,30},{18,... | collective-permute-start | bytes 196616 | tf_op jit(solution)/shard_map/ppermute | solution.py:43
  26.2 0.5 %collective-permute-start.9 = (f32[2,64,128]{2,1,0:T(8,128)S(1)}, f32[2,64,128]{2,1,0:T(8,128)S(1)}, u32[]{:S(2)}, u32[]{:S(2)}) collective-permute-start(f32[2,64,128]{2,1,0:T(8,128)S(1)} %get-tuple-element.29), channel_id=1, source_target_pairs={{0,6},{2,4},{4,2},{6,0},{8,14},{10,12},{12,10},{14,8},{16,22},{18,... | collective-permute-start | bytes 196616 | tf_op jit(solution)/shard_map/ppermute | solution.py:43
  26.7 1.2 %collective-permute-start.8 = (f32[2,64,128]{2,1,0:T(8,128)S(1)}, f32[2,64,128]{2,1,0:T(8,128)S(1)}, u32[]{:S(2)}, u32[]{:S(2)}) collective-permute-start(f32[2,64,128]{2,1,0:T(8,128)S(1)} %get-tuple-element.30), channel_id=1, source_target_pairs={{0,10},{2,8},{4,14},{6,12},{8,2},{10,0},{12,6},{14,4},{16,26},{18,... | collective-permute-start | bytes 196616 | tf_op jit(solution)/shard_map/ppermute | solution.py:43
  27.9 2.1 %collective-permute-done.7 = f32[2,64,128]{2,1,0:T(8,128)S(1)} collective-permute-done((f32[2,64,128]{2,1,0:T(8,128)S(1)}, f32[2,64,128]{2,1,0:T(8,128)S(1)}, u32[]{:S(2)}, u32[]{:S(2)}) %collective-permute-start.7) | collective-permute-done | bytes 65568 | tf_op jit(solution)/shard_map/ppermute | solution.py:43
  30.0 1.6 %collective-permute-done.9 = f32[2,64,128]{2,1,0:T(8,128)S(1)} collective-permute-done((f32[2,64,128]{2,1,0:T(8,128)S(1)}, f32[2,64,128]{2,1,0:T(8,128)S(1)}, u32[]{:S(2)}, u32[]{:S(2)}) %collective-permute-start.9) | collective-permute-done | bytes 65568 | tf_op jit(solution)/shard_map/ppermute | solution.py:43
  31.6 0.0 collective-permute-done.8
  31.6 2.8 %collective-permute-start.10 = (f32[1,64,128]{2,1,0:T(8,128)S(1)}, f32[1,64,128]{2,1,0:T(8,128)S(1)}, u32[]{:S(2)}, u32[]{:S(2)}) collective-permute-start(f32[1,64,128]{2,1,0:T(8,128)S(1)} %split.29), channel_id=1, source_target_pairs={{0,18},{2,16},{4,22},{6,20},{8,26},{10,24},{12,30},{14,28},{16,2},... | collective-permute-start | bytes 98312 | tf_op jit(solution)/shard_map/ppermute | solution.py:43
  34.4 0.6 %convert_element_type.15 = bf16[16,16,128]{2,1,0:T(8,128)(2,1)} convert(f32[16,16,128]{2,1,0:T(8,128)S(1)} %get-tuple-element.27) | non-fusion elementwise | flops 32768 | bytes 196608 | tf_op jit(solution)/shard_map/convert_element_type | solution.py:259
  35.0 1.8 %collective-permute-done.10 = f32[1,64,128]{2,1,0:T(8,128)S(1)} collective-permute-done((f32[1,64,128]{2,1,0:T(8,128)S(1)}, f32[1,64,128]{2,1,0:T(8,128)S(1)}, u32[]{:S(2)}, u32[]{:S(2)}) %collective-permute-start.10) | collective-permute-done | bytes 32800 | tf_op jit(solution)/shard_map/ppermute | solution.py:43
  36.8 0.6 %fusion.2 = f32[1,1,64,128]{3,2,1,0:T(8,128)} fusion(f32[1,64,128]{2,1,0:T(8,128)S(1)} %collective-permute-done.10, f32[2,64,128]{2,1,0:T(8,128)S(1)} %fusion.1), kind=kLoop, calls=%fused_computation.5 | loop fusion | flops 8192 | bytes 98304 | tf_op jit(solution)/shard_map/broadcast_in_dim | solution.py:259
  (11 shorter events, 0.1 us)
Async XLA Ops:
  0.6 5.2 %collective-permute-start = (bf16[1,64,128]{2,1,0:T(8,128)(2,1)}, bf16[1,64,128]{2,1,0:T(8,128)(2,1)S(1)}, u32[]{:S(2)}, u32[]{:S(2)}) collective-permute-start(bf16[1,64,128]{2,1,0:T(8,128)(2,1)} %bitcast.5), channel_id=1, source_target_pairs={{0,18},{2,16},{4,22},{6,20},{8,26},{10,24},{12,30},{14,28},{16,2},... | collective-permute-start | bytes 49160 | tf_op jit(solution)/shard_map/ppermute | solution.py:43
  5.8 6.5 %collective-permute-start.3 = (bf16[2,64,128]{2,1,0:T(8,128)(2,1)S(1)}, bf16[2,64,128]{2,1,0:T(8,128)(2,1)S(1)}, u32[]{:S(2)}, u32[]{:S(2)}) collective-permute-start(bf16[2,64,128]{2,1,0:T(8,128)(2,1)S(1)} %constant_dynamic-update-slice_fusion.4.gate_ref), channel_id=1, source_target_pairs={{0,6},{2,4},{4,2},{6,0},{8,14},{10,12},{12,10},{14,8},{16,22},{18,... | collective-permute-start | bytes 98312 | tf_op jit(solution)/shard_map/ppermute | solution.py:43
  7.6 4.7 %collective-permute-start.2 = (bf16[2,64,128]{2,1,0:T(8,128)(2,1)S(1)}, bf16[2,64,128]{2,1,0:T(8,128)(2,1)S(1)}, u32[]{:S(2)}, u32[]{:S(2)}) collective-permute-start(bf16[2,64,128]{2,1,0:T(8,128)(2,1)S(1)} %constant_dynamic-update-slice_fusion.4.gate_ref), channel_id=1, source_target_pairs={{0,10},{2,8},{4,14},{6,12},{8,2},{10,0},{12,6},{14,4},{16,26},{18,... | collective-permute-start | bytes 98312 | tf_op jit(solution)/shard_map/ppermute | solution.py:43
  9.2 4.3 %collective-permute-start.1 = (bf16[2,64,128]{2,1,0:T(8,128)(2,1)S(1)}, bf16[2,64,128]{2,1,0:T(8,128)(2,1)S(1)}, u32[]{:S(2)}, u32[]{:S(2)}) collective-permute-start(bf16[2,64,128]{2,1,0:T(8,128)(2,1)S(1)} %constant_dynamic-update-slice_fusion.4.gate_ref), channel_id=1, source_target_pairs={{0,14},{2,12},{4,10},{6,8},{8,6},{10,4},{12,2},{14,0},{16,30},{18,... | collective-permute-start | bytes 98312 | tf_op jit(solution)/shard_map/ppermute | solution.py:43
  13.6 1.4 %collective-permute-start.4 = (bf16[8,64,128]{2,1,0:T(8,128)(2,1)S(1)}, bf16[8,64,128]{2,1,0:T(8,128)(2,1)S(1)}, u32[]{:S(2)}, u32[]{:S(2)}) collective-permute-start(bf16[8,64,128]{2,1,0:T(8,128)(2,1)S(1)} %constant_dynamic-update-slice_fusion.mine_ref), channel_id=1, source_target_pairs={{0,2},{2,0},{4,6},{6,4},{8,10},{10,8},{12,14},{14,12},{16,18},{18,... | collective-permute-start | bytes 393224 | tf_op jit(solution)/shard_map/ppermute | solution.py:43
  17.2 4.3 %collective-permute-start.5 = (f16[16,16,128]{2,1,0:T(8,128)(2,1)S(1)}, f16[16,16,128]{2,1,0:T(8,128)(2,1)S(1)}, u32[]{:S(2)}, u32[]{:S(2)}) collective-permute-start(f16[16,16,128]{2,1,0:T(8,128)(2,1)S(1)} %convert_element_type.12), channel_id=1, source_target_pairs={{0,1},{1,0},{2,3},{3,2},{4,5},{5,4},{6,7},{7,6},{8,9},{9,8},{10,11... | collective-permute-start | bytes 196616 | tf_op jit(solution)/shard_map/ppermute | solution.py:43
  23.2 1.6 %collective-permute-start.6 = (f32[8,64,128]{2,1,0:T(8,128)S(1)}, f32[8,64,128]{2,1,0:T(8,128)S(1)}, u32[]{:S(2)}, u32[]{:S(2)}) collective-permute-start(f32[8,64,128]{2,1,0:T(8,128)S(1)} %get-tuple-element.26), channel_id=1, source_target_pairs={{0,2},{2,0},{4,6},{6,4},{8,10},{10,8},{12,14},{14,12},{16,18},{18,... | collective-permute-start | bytes 786440 | tf_op jit(solution)/shard_map/ppermute | solution.py:43
  24.9 5.1 %collective-permute-start.7 = (f32[2,64,128]{2,1,0:T(8,128)S(1)}, f32[2,64,128]{2,1,0:T(8,128)S(1)}, u32[]{:S(2)}, u32[]{:S(2)}) collective-permute-start(f32[2,64,128]{2,1,0:T(8,128)S(1)} %get-tuple-element.28), channel_id=1, source_target_pairs={{0,14},{2,12},{4,10},{6,8},{8,6},{10,4},{12,2},{14,0},{16,30},{18,... | collective-permute-start | bytes 196616 | tf_op jit(solution)/shard_map/ppermute | solution.py:43
  26.2 5.4 %collective-permute-start.9 = (f32[2,64,128]{2,1,0:T(8,128)S(1)}, f32[2,64,128]{2,1,0:T(8,128)S(1)}, u32[]{:S(2)}, u32[]{:S(2)}) collective-permute-start(f32[2,64,128]{2,1,0:T(8,128)S(1)} %get-tuple-element.29), channel_id=1, source_target_pairs={{0,6},{2,4},{4,2},{6,0},{8,14},{10,12},{12,10},{14,8},{16,22},{18,... | collective-permute-start | bytes 196616 | tf_op jit(solution)/shard_map/ppermute | solution.py:43
  26.7 4.9 %collective-permute-start.8 = (f32[2,64,128]{2,1,0:T(8,128)S(1)}, f32[2,64,128]{2,1,0:T(8,128)S(1)}, u32[]{:S(2)}, u32[]{:S(2)}) collective-permute-start(f32[2,64,128]{2,1,0:T(8,128)S(1)} %get-tuple-element.30), channel_id=1, source_target_pairs={{0,10},{2,8},{4,14},{6,12},{8,2},{10,0},{12,6},{14,4},{16,26},{18,... | collective-permute-start | bytes 196616 | tf_op jit(solution)/shard_map/ppermute | solution.py:43
  31.6 5.2 %collective-permute-start.10 = (f32[1,64,128]{2,1,0:T(8,128)S(1)}, f32[1,64,128]{2,1,0:T(8,128)S(1)}, u32[]{:S(2)}, u32[]{:S(2)}) collective-permute-start(f32[1,64,128]{2,1,0:T(8,128)S(1)} %split.29), channel_id=1, source_target_pairs={{0,18},{2,16},{4,22},{6,20},{8,26},{10,24},{12,30},{14,28},{16,2},... | collective-permute-start | bytes 98312 | tf_op jit(solution)/shard_map/ppermute | solution.py:43

commit v4 on v3

--- a/solution.py
+++ b/solution.py
@@ -1,4 +1,5 @@
 import functools
+import math
 
 import jax
 import jax.numpy as jnp
@@ -113,8 +114,8 @@
         rows = jnp.concatenate([flux_ref[place_ref[j, tile]] for j in range(per_tile)], axis=1)
         sens = jnp.concatenate([print_ref[tile, j] for j in range(per_tile)], axis=1)
         total = lax.dot_general(
-            rows, sens, (((1,), (1,)), ((), ())), preferred_element_type=jnp.float32
-        )
+            sens, rows, (((1,), (1,)), ((), ())), preferred_element_type=jnp.float32
+        ).T
         weeks = weeks_ref[pl.ds(tile, 1), :]
         picked = total[:MEMBERS]
         for week in range(1, WEEKS):
@@ -250,12 +251,22 @@
         compiler_params=params,
         name="adjoint",
     )(place, weeks, modeled, shift, scale, held)
-    total = keep + swap(send, "obs", devices, 1)
+    peak = slots * per_tile * sounds * 0.125 * 3.0 * 1548.0
+
+    def swap_sum(value, added, mask):
+        scale = 2.0 ** math.ceil(math.log2(peak * added / 65504.0))
+        sent = (value * (1.0 / scale)).astype(jnp.float16)
+        return swap(sent, "obs", devices, mask).astype(jnp.float32) * scale
+
+    added = 1
+    total = keep + swap_sum(send, added, 1)
+    added *= 2
     for masks in rounds[::-1]:
         pieces = jnp.split(total, len(masks) + 1, axis=0)
         total = pieces[0]
         for mask, piece in zip(masks, pieces[1:]):
-            total = total + swap(piece, "obs", devices, mask)
+            total = total + swap_sum(piece, added, mask)
+        added *= len(masks) + 1
     return (total[None], residual.astype(jnp.bfloat16))
 
 

time: 37.8 us -> 35 us (0.926)
  waiting for transfers between devices: 13.1 us -> 10.3 us
    ppermute x11, waiting for transfers between devices: 13.1 us -> 10.3 us  [swap(): return lax.ppermute(value, axis, [(i, i ^ mask) for i in range(count)])]
  transfers between devices with their start and end apart: 11 -> 11, of which waited for: 8 -> 8; matrix products, arithmetic and copies ran while one was open for 4% -> 4% of each run, Pallas kernels for 6% -> 7%
where the time goes in v4:
time: 35 us; the launch traced here: 34.6 us
  starting transfers between devices  14.7 us (42%)
  waiting for transfers between devices  10.3 us (29%)
  Pallas kernels  5.9 us (17%)
  other arithmetic  2.21 us (6%)
  between operations  1.39 us (4%)
    ppermute x11, starting transfers between devices, swap(): return lax.ppermute(value, axis, [(i, i ^ mask) for i in range(count)])  14.7 us
    ppermute x11, waiting for transfers between devices, swap(): return lax.ppermute(value, axis, [(i, i ^ mask) for i in range(count)])  10.3 us
    pallas_call x1, Pallas kernels, on_device(): pl.pallas_call(functools.partial(prepare_kernel, rounds), out_shape=(shap...  2.36 us
    pallas_call x1, Pallas kernels, on_device(): pl.pallas_call(forward_kernel, out_shape=shape((slots, MEMBERS, sounds),...  1.91 us
    pallas_call x1, Pallas kernels, on_device(): pl.pallas_call(adjoint_kernel, out_shape=(shape((half, ROWS, cells), jnp....  1.63 us
    concatenate x1, other arithmetic, on_device(): jnp.concatenate([have] * (len(masks) + 1), axis=0)  0.79 us
  transfers between devices with their start and end apart: 11, of which 8 were waited for; matrix products, arithmetic and copies ran while one was open for 4% of the time, Pallas kernels for 7%

profile of v4, /device:TPU:0, one launch (start us, length us, event | category | flops | bytes accessed | tf_op | source)
XLA Modules:
  0.0 34.6 jit_solution(187140423861319174)
XLA Ops:
  0.6 3.5 %collective-permute-start = (bf16[1,64,128]{2,1,0:T(8,128)(2,1)}, bf16[1,64,128]{2,1,0:T(8,128)(2,1)S(1)}, u32[]{:S(2)}, u32[]{:S(2)}) collective-permute-start(bf16[1,64,128]{2,1,0:T(8,128)(2,1)} %bitcast.5), channel_id=1, source_target_pairs={{0,18},{2,16},{4,22},{6,20},{8,26},{10,24},{12,30},{14,28},{16,2},... | collective-permute-start | bytes 49160 | tf_op jit(solution)/shard_map/ppermute | solution.py:44
  4.2 0.8 %pad_maximum_fusion = bf16[2,64,128]{2,1,0:T(8,128)(2,1)S(1)} fusion(bf16[1,64,128]{2,1,0:T(8,128)(2,1)} %bitcast.6), kind=kLoop, calls=%fused_computation.16 | loop fusion | flops 16384 | bytes 49152 | tf_op jit(solution)/shard_map/concatenate | solution.py:187
  5.0 0.9 %collective-permute-done = bf16[1,64,128]{2,1,0:T(8,128)(2,1)S(1)} collective-permute-done((bf16[1,64,128]{2,1,0:T(8,128)(2,1)}, bf16[1,64,128]{2,1,0:T(8,128)(2,1)S(1)}, u32[]{:S(2)}, u32[]{:S(2)}) %collective-permute-start) | collective-permute-done | bytes 16416 | tf_op jit(solution)/shard_map/ppermute | solution.py:44
  5.8 1.8 %collective-permute-start.3 = (bf16[2,64,128]{2,1,0:T(8,128)(2,1)S(1)}, bf16[2,64,128]{2,1,0:T(8,128)(2,1)S(1)}, u32[]{:S(2)}, u32[]{:S(2)}) collective-permute-start(bf16[2,64,128]{2,1,0:T(8,128)(2,1)S(1)} %constant_dynamic-update-slice_fusion.4.gate_ref), channel_id=1, source_target_pairs={{0,6},{2,4},{4,2},{6,0},{8,14},{10,12},{12,10},{14,8},{16,22},{18,... | collective-permute-start | bytes 98312 | tf_op jit(solution)/shard_map/ppermute | solution.py:44
  7.6 1.6 %collective-permute-start.2 = (bf16[2,64,128]{2,1,0:T(8,128)(2,1)S(1)}, bf16[2,64,128]{2,1,0:T(8,128)(2,1)S(1)}, u32[]{:S(2)}, u32[]{:S(2)}) collective-permute-start(bf16[2,64,128]{2,1,0:T(8,128)(2,1)S(1)} %constant_dynamic-update-slice_fusion.4.gate_ref), channel_id=1, source_target_pairs={{0,10},{2,8},{4,14},{6,12},{8,2},{10,0},{12,6},{14,4},{16,26},{18,... | collective-permute-start | bytes 98312 | tf_op jit(solution)/shard_map/ppermute | solution.py:44
  9.2 0.1 collective-permute-start.1
  10.0 2.4 %prepare.1 = (s32[8,16]{1,0:T(8,128)S(1)}, s32[16,128]{1,0:T(8,128)S(1)}, f32[16,16,128]{2,1,0:T(8,128)S(1)}, f32[16,128]{1,0:T(8,128)S(1)}, bf16[16,8,128,128]{3,2,1,0:T(8,128)(2,1)S(1)}) custom-call(bf16[2,64,128]{2,1,0:T(8,128)(2,1)S(1)} %constant_dynamic-update-slice_fusion.4.gate_ref, s32[1]{0:T(128)S(6)} %copy.15.count_ref, s32[8,16]{1,0:T(8,128)} %bitcast.7, ...), custom_call_target="tpu_custom_call" | custom-call | bytes 8388608 | tf_op jit(solution)/shard_map/prepare/pallas_call | solution.py:200
  12.3 0.0 collective-permute-done.3
  12.3 0.0 collective-permute-done.2
  12.3 1.2 %collective-permute-done.1 = bf16[2,64,128]{2,1,0:T(8,128)(2,1)S(1)} collective-permute-done((bf16[2,64,128]{2,1,0:T(8,128)(2,1)S(1)}, bf16[2,64,128]{2,1,0:T(8,128)(2,1)S(1)}, u32[]{:S(2)}, u32[]{:S(2)}) %collective-permute-start.1) | collective-permute-done | bytes 32800 | tf_op jit(solution)/shard_map/ppermute | solution.py:44
  13.6 0.2 collective-permute-start.4
  13.8 1.2 %collective-permute-done.4.other_ref = bf16[8,64,128]{2,1,0:T(8,128)(2,1)S(1)} collective-permute-done((bf16[8,64,128]{2,1,0:T(8,128)(2,1)S(1)}, bf16[8,64,128]{2,1,0:T(8,128)(2,1)S(1)}, u32[]{:S(2)}, u32[]{:S(2)}) %collective-permute-start.4) | collective-permute-done | bytes 131104 | tf_op jit(solution)/shard_map/ppermute | solution.py:44
  15.0 1.9 %forward.1 = f32[16,16,128]{2,1,0:T(8,128)S(1)} custom-call(s32[8,16]{1,0:T(8,128)S(1)} %get-tuple-element.15.place_ref, s32[16,128]{1,0:T(8,128)S(1)} %get-tuple-element.16.weeks_ref, bf16[8,64,128]{2,1,0:T(8,128)(2,1)S(1)} %constant_dynamic-update-slice_fusion.mine_ref, bf16[8,64,128]{2,1,0:T(8,128)(2,1)S(1)} %collective-permute-done.4.other_ref, ...), custom_call_target="tpu_custom_call" | custom-call | tf_op jit(solution)/shard_map/forward/pallas_call | solution.py:225
  17.0 1.6 %collective-permute-start.5 = (f16[16,16,128]{2,1,0:T(8,128)(2,1)S(1)}, f16[16,16,128]{2,1,0:T(8,128)(2,1)S(1)}, u32[]{:S(2)}, u32[]{:S(2)}) collective-permute-start(f16[16,16,128]{2,1,0:T(8,128)(2,1)S(1)} %convert_element_type.42), channel_id=1, source_target_pairs={{0,1},{1,0},{2,3},{3,2},{4,5},{5,4},{6,7},{7,6},{8,9},{9,8},{10,11... | collective-permute-start | bytes 196616 | tf_op jit(solution)/shard_map/ppermute | solution.py:44
  18.6 2.7 %collective-permute-done.5 = f16[16,16,128]{2,1,0:T(8,128)(2,1)S(1)} collective-permute-done((f16[16,16,128]{2,1,0:T(8,128)(2,1)S(1)}, f16[16,16,128]{2,1,0:T(8,128)(2,1)S(1)}, u32[]{:S(2)}, u32[]{:S(2)}) %collective-permute-start.5) | collective-permute-done | bytes 65568 | tf_op jit(solution)/shard_map/ppermute | solution.py:44
  21.3 1.6 %adjoint.1 = (f32[8,64,128]{2,1,0:T(8,128)S(1)}, f32[8,64,128]{2,1,0:T(8,128)S(1)}, f32[16,16,128]{2,1,0:T(8,128)S(1)}) custom-call(s32[8,16]{1,0:T(8,128)S(1)} %get-tuple-element.15.place_ref, s32[16,128]{1,0:T(8,128)S(1)} %get-tuple-element.16.weeks_ref, f32[16,16,128]{2,1,0:T(8,128)S(1)} %convert_add_fusion.modeled_ref, ...), custom_call_target="tpu_custom_call" | custom-call | tf_op jit(solution)/shard_map/adjoint/pallas_call | solution.py:241
  23.0 0.1 collective-permute-start.6
  23.1 1.3 %collective-permute-done.6 = f16[8,64,128]{2,1,0:T(8,128)(2,1)S(1)} collective-permute-done((f16[8,64,128]{2,1,0:T(8,128)(2,1)S(1)}, f16[8,64,128]{2,1,0:T(8,128)(2,1)S(1)}, u32[]{:S(2)}, u32[]{:S(2)}) %collective-permute-start.6) | collective-permute-done | bytes 131104 | tf_op jit(solution)/shard_map/ppermute | solution.py:44
  24.5 1.3 %collective-permute-start.7 = (f16[2,64,128]{2,1,0:T(8,128)(2,1)S(1)}, f16[2,64,128]{2,1,0:T(8,128)(2,1)S(1)}, u32[]{:S(2)}, u32[]{:S(2)}) collective-permute-start(f16[2,64,128]{2,1,0:T(8,128)(2,1)S(1)} %get-tuple-element.28), channel_id=1, source_target_pairs={{0,14},{2,12},{4,10},{6,8},{8,6},{10,4},{12,2},{14,0},{16,30},{18,... | collective-permute-start | bytes 98312 | tf_op jit(solution)/shard_map/ppermute | solution.py:44
  25.8 0.5 %collective-permute-start.9 = (f16[2,64,128]{2,1,0:T(8,128)(2,1)S(1)}, f16[2,64,128]{2,1,0:T(8,128)(2,1)S(1)}, u32[]{:S(2)}, u32[]{:S(2)}) collective-permute-start(f16[2,64,128]{2,1,0:T(8,128)(2,1)S(1)} %get-tuple-element.29), channel_id=1, source_target_pairs={{0,6},{2,4},{4,2},{6,0},{8,14},{10,12},{12,10},{14,8},{16,22},{18,... | collective-permute-start | bytes 98312 | tf_op jit(solution)/shard_map/ppermute | solution.py:44
  26.3 1.2 %collective-permute-start.8 = (f16[2,64,128]{2,1,0:T(8,128)(2,1)S(1)}, f16[2,64,128]{2,1,0:T(8,128)(2,1)S(1)}, u32[]{:S(2)}, u32[]{:S(2)}) collective-permute-start(f16[2,64,128]{2,1,0:T(8,128)(2,1)S(1)} %get-tuple-element.30), channel_id=1, source_target_pairs={{0,10},{2,8},{4,14},{6,12},{8,2},{10,0},{12,6},{14,4},{16,26},{18,... | collective-permute-start | bytes 98312 | tf_op jit(solution)/shard_map/ppermute | solution.py:44
  27.5 1.3 %collective-permute-done.7 = f16[2,64,128]{2,1,0:T(8,128)(2,1)S(1)} collective-permute-done((f16[2,64,128]{2,1,0:T(8,128)(2,1)S(1)}, f16[2,64,128]{2,1,0:T(8,128)(2,1)S(1)}, u32[]{:S(2)}, u32[]{:S(2)}) %collective-permute-start.7) | collective-permute-done | bytes 32800 | tf_op jit(solution)/shard_map/ppermute | solution.py:44
  28.8 0.8 %collective-permute-done.9 = f16[2,64,128]{2,1,0:T(8,128)(2,1)S(1)} collective-permute-done((f16[2,64,128]{2,1,0:T(8,128)(2,1)S(1)}, f16[2,64,128]{2,1,0:T(8,128)(2,1)S(1)}, u32[]{:S(2)}, u32[]{:S(2)}) %collective-permute-start.9) | collective-permute-done | bytes 32800 | tf_op jit(solution)/shard_map/ppermute | solution.py:44
  29.6 0.0 collective-permute-done.8
  29.7 2.8 %collective-permute-start.10 = (f16[1,64,128]{2,1,0:T(8,128)(2,1)S(1)}, f16[1,64,128]{2,1,0:T(8,128)(2,1)S(1)}, u32[]{:S(2)}, u32[]{:S(2)}) collective-permute-start(f16[1,64,128]{2,1,0:T(8,128)(2,1)S(1)} %fusion.5), channel_id=1, source_target_pairs={{0,18},{2,16},{4,22},{6,20},{8,26},{10,24},{12,30},{14,28},{16,2},... | collective-permute-start | bytes 49160 | tf_op jit(solution)/shard_map/ppermute | solution.py:44
  32.5 0.6 %convert_element_type.55 = bf16[16,16,128]{2,1,0:T(8,128)(2,1)} convert(f32[16,16,128]{2,1,0:T(8,128)S(1)} %get-tuple-element.27) | non-fusion elementwise | flops 32768 | bytes 196608 | tf_op jit(solution)/shard_map/convert_element_type | solution.py:270
  33.2 0.8 %collective-permute-done.10 = f16[1,64,128]{2,1,0:T(8,128)(2,1)S(1)} collective-permute-done((f16[1,64,128]{2,1,0:T(8,128)(2,1)S(1)}, f16[1,64,128]{2,1,0:T(8,128)(2,1)S(1)}, u32[]{:S(2)}, u32[]{:S(2)}) %collective-permute-start.10) | collective-permute-done | bytes 16416 | tf_op jit(solution)/shard_map/ppermute | solution.py:44
  34.0 0.6 %fusion.6 = f32[1,1,64,128]{3,2,1,0:T(8,128)} fusion(f32[2,64,128]{2,1,0:T(8,128)S(1)} %fusion.4, f16[1,64,128]{2,1,0:T(8,128)(2,1)S(1)} %collective-permute-done.10), kind=kLoop, calls=%fused_computation.15 | loop fusion | flops 24576 | bytes 81920 | tf_op jit(solution)/shard_map/broadcast_in_dim | solution.py:270
  (12 shorter events, 0.2 us)
Async XLA Ops:
  0.6 5.2 %collective-permute-start = (bf16[1,64,128]{2,1,0:T(8,128)(2,1)}, bf16[1,64,128]{2,1,0:T(8,128)(2,1)S(1)}, u32[]{:S(2)}, u32[]{:S(2)}) collective-permute-start(bf16[1,64,128]{2,1,0:T(8,128)(2,1)} %bitcast.5), channel_id=1, source_target_pairs={{0,18},{2,16},{4,22},{6,20},{8,26},{10,24},{12,30},{14,28},{16,2},... | collective-permute-start | bytes 49160 | tf_op jit(solution)/shard_map/ppermute | solution.py:44
  5.8 6.5 %collective-permute-start.3 = (bf16[2,64,128]{2,1,0:T(8,128)(2,1)S(1)}, bf16[2,64,128]{2,1,0:T(8,128)(2,1)S(1)}, u32[]{:S(2)}, u32[]{:S(2)}) collective-permute-start(bf16[2,64,128]{2,1,0:T(8,128)(2,1)S(1)} %constant_dynamic-update-slice_fusion.4.gate_ref), channel_id=1, source_target_pairs={{0,6},{2,4},{4,2},{6,0},{8,14},{10,12},{12,10},{14,8},{16,22},{18,... | collective-permute-start | bytes 98312 | tf_op jit(solution)/shard_map/ppermute | solution.py:44
  7.6 4.7 %collective-permute-start.2 = (bf16[2,64,128]{2,1,0:T(8,128)(2,1)S(1)}, bf16[2,64,128]{2,1,0:T(8,128)(2,1)S(1)}, u32[]{:S(2)}, u32[]{:S(2)}) collective-permute-start(bf16[2,64,128]{2,1,0:T(8,128)(2,1)S(1)} %constant_dynamic-update-slice_fusion.4.gate_ref), channel_id=1, source_target_pairs={{0,10},{2,8},{4,14},{6,12},{8,2},{10,0},{12,6},{14,4},{16,26},{18,... | collective-permute-start | bytes 98312 | tf_op jit(solution)/shard_map/ppermute | solution.py:44
  9.2 4.3 %collective-permute-start.1 = (bf16[2,64,128]{2,1,0:T(8,128)(2,1)S(1)}, bf16[2,64,128]{2,1,0:T(8,128)(2,1)S(1)}, u32[]{:S(2)}, u32[]{:S(2)}) collective-permute-start(bf16[2,64,128]{2,1,0:T(8,128)(2,1)S(1)} %constant_dynamic-update-slice_fusion.4.gate_ref), channel_id=1, source_target_pairs={{0,14},{2,12},{4,10},{6,8},{8,6},{10,4},{12,2},{14,0},{16,30},{18,... | collective-permute-start | bytes 98312 | tf_op jit(solution)/shard_map/ppermute | solution.py:44
  13.6 1.4 %collective-permute-start.4 = (bf16[8,64,128]{2,1,0:T(8,128)(2,1)S(1)}, bf16[8,64,128]{2,1,0:T(8,128)(2,1)S(1)}, u32[]{:S(2)}, u32[]{:S(2)}) collective-permute-start(bf16[8,64,128]{2,1,0:T(8,128)(2,1)S(1)} %constant_dynamic-update-slice_fusion.mine_ref), channel_id=1, source_target_pairs={{0,2},{2,0},{4,6},{6,4},{8,10},{10,8},{12,14},{14,12},{16,18},{18,... | collective-permute-start | bytes 393224 | tf_op jit(solution)/shard_map/ppermute | solution.py:44
  17.0 4.3 %collective-permute-start.5 = (f16[16,16,128]{2,1,0:T(8,128)(2,1)S(1)}, f16[16,16,128]{2,1,0:T(8,128)(2,1)S(1)}, u32[]{:S(2)}, u32[]{:S(2)}) collective-permute-start(f16[16,16,128]{2,1,0:T(8,128)(2,1)S(1)} %convert_element_type.42), channel_id=1, source_target_pairs={{0,1},{1,0},{2,3},{3,2},{4,5},{5,4},{6,7},{7,6},{8,9},{9,8},{10,11... | collective-permute-start | bytes 196616 | tf_op jit(solution)/shard_map/ppermute | solution.py:44
  23.0 1.4 %collective-permute-start.6 = (f16[8,64,128]{2,1,0:T(8,128)(2,1)S(1)}, f16[8,64,128]{2,1,0:T(8,128)(2,1)S(1)}, u32[]{:S(2)}, u32[]{:S(2)}) collective-permute-start(f16[8,64,128]{2,1,0:T(8,128)(2,1)S(1)} %multiply_convert_fusion), channel_id=1, source_target_pairs={{0,2},{2,0},{4,6},{6,4},{8,10},{10,8},{12,14},{14,12},{16,18},{18,... | collective-permute-start | bytes 393224 | tf_op jit(solution)/shard_map/ppermute | solution.py:44
  24.5 4.3 %collective-permute-start.7 = (f16[2,64,128]{2,1,0:T(8,128)(2,1)S(1)}, f16[2,64,128]{2,1,0:T(8,128)(2,1)S(1)}, u32[]{:S(2)}, u32[]{:S(2)}) collective-permute-start(f16[2,64,128]{2,1,0:T(8,128)(2,1)S(1)} %get-tuple-element.28), channel_id=1, source_target_pairs={{0,14},{2,12},{4,10},{6,8},{8,6},{10,4},{12,2},{14,0},{16,30},{18,... | collective-permute-start | bytes 98312 | tf_op jit(solution)/shard_map/ppermute | solution.py:44
  25.8 3.8 %collective-permute-start.9 = (f16[2,64,128]{2,1,0:T(8,128)(2,1)S(1)}, f16[2,64,128]{2,1,0:T(8,128)(2,1)S(1)}, u32[]{:S(2)}, u32[]{:S(2)}) collective-permute-start(f16[2,64,128]{2,1,0:T(8,128)(2,1)S(1)} %get-tuple-element.29), channel_id=1, source_target_pairs={{0,6},{2,4},{4,2},{6,0},{8,14},{10,12},{12,10},{14,8},{16,22},{18,... | collective-permute-start | bytes 98312 | tf_op jit(solution)/shard_map/ppermute | solution.py:44
  26.3 3.3 %collective-permute-start.8 = (f16[2,64,128]{2,1,0:T(8,128)(2,1)S(1)}, f16[2,64,128]{2,1,0:T(8,128)(2,1)S(1)}, u32[]{:S(2)}, u32[]{:S(2)}) collective-permute-start(f16[2,64,128]{2,1,0:T(8,128)(2,1)S(1)} %get-tuple-element.30), channel_id=1, source_target_pairs={{0,10},{2,8},{4,14},{6,12},{8,2},{10,0},{12,6},{14,4},{16,26},{18,... | collective-permute-start | bytes 98312 | tf_op jit(solution)/shard_map/ppermute | solution.py:44
  29.7 4.3 %collective-permute-start.10 = (f16[1,64,128]{2,1,0:T(8,128)(2,1)S(1)}, f16[1,64,128]{2,1,0:T(8,128)(2,1)S(1)}, u32[]{:S(2)}, u32[]{:S(2)}) collective-permute-start(f16[1,64,128]{2,1,0:T(8,128)(2,1)S(1)} %fusion.5), channel_id=1, source_target_pairs={{0,18},{2,16},{4,22},{6,20},{8,26},{10,24},{12,30},{14,28},{16,2},... | collective-permute-start | bytes 49160 | tf_op jit(solution)/shard_map/ppermute | solution.py:44

commit v5 on v4

--- a/solution.py
+++ b/solution.py
@@ -47,7 +47,6 @@
 def prepare_kernel(
     rounds,
     gate_ref,
-    count_ref,
     blocks_hbm,
     ids_hbm,
     weeks_hbm,
@@ -58,13 +57,12 @@
     place_ref,
     weeks_ref,
     shift_ref,
-    scale_ref,
+    weight_ref,
     held_ref,
     blocks_ref,
     ids_ref,
     seen_ref,
     noise_ref,
-    weight_ref,
     sems,
 ):
     pairs = (
@@ -100,8 +98,6 @@
     for tile in range(shift_ref.shape[0]):
         shifted = jnp.dot(hot, noise_ref[tile], preferred_element_type=jnp.float32)
         shift_ref[tile] = seen_ref[pl.ds(tile, 1), :] + shifted
-    alive = lax.broadcasted_iota(jnp.int32, weight_ref.shape, 0) < count_ref[0]
-    scale_ref[...] = jnp.where(alive, jnp.float32(1), jnp.float32(0)) * weight_ref[...]
     copies[-1].wait()
 
 
@@ -124,11 +120,12 @@
 
 
 def adjoint_kernel(
+    count_ref,
     place_ref,
     weeks_ref,
     modeled_ref,
     shift_ref,
-    scale_ref,
+    weight_ref,
     print_ref,
     keep_ref,
     send_ref,
@@ -138,10 +135,12 @@
 ):
     slots, per_tile = print_ref.shape[:2]
     sums = (first_ref, second_ref)
+    count = count_ref[0]
     for total_ref in sums:
         total_ref[...] = jnp.zeros_like(total_ref)
     for tile in range(slots):
-        residual = scale_ref[pl.ds(tile, 1), :] * (modeled_ref[tile] - shift_ref[tile])
+        alive = jnp.where(tile < count, jnp.float32(1), jnp.float32(0))
+        residual = (alive * weight_ref[pl.ds(tile, 1), :]) * (modeled_ref[tile] - shift_ref[tile])
         residual_ref[tile] = residual
         weeks = weeks_ref[pl.ds(tile, 1), :]
         rows = jnp.concatenate(
@@ -195,9 +194,9 @@
         (sounding_week, None),
         (observed, pltpu.VMEM),
         (perturb, pltpu.VMEM),
-        (obs_weight, pltpu.VMEM),
-    )
-    place, weeks, shift, scale, held = pl.pallas_call(
+        (obs_weight, None),
+    )
+    place, weeks, shift, weight, held = pl.pallas_call(
         functools.partial(prepare_kernel, rounds),
         out_shape=(
             shape((per_tile, slots), jnp.int32),
@@ -206,7 +205,7 @@
             shape((slots, sounds), jnp.float32),
             shape(footprint.shape, footprint.dtype),
         ),
-        in_specs=[VMEM, SMEM] + [HBM] * 7,
+        in_specs=[VMEM] + [HBM] * 7,
         out_specs=(VMEM,) * 5,
         scratch_shapes=[kind(x.shape, x.dtype) for x, kind in small if kind]
         + [pltpu.SemaphoreType.DMA((7,))],
@@ -215,7 +214,6 @@
         name="prepare",
     )(
         gate,
-        tile_count,
         *[pltpu.with_memory_space_constraint(x, pltpu.HBM) for x, _ in small],
         pltpu.with_memory_space_constraint(footprint, pltpu.HBM),
     )
@@ -245,12 +243,12 @@
             shape((half, ROWS, cells), jnp.float32),
             shape((slots, MEMBERS, sounds), jnp.float32),
         ),
-        in_specs=[SMEM] + [VMEM] * 5,
+        in_specs=[SMEM, SMEM] + [VMEM] * 5,
         out_specs=(VMEM, VMEM, VMEM),
         scratch_shapes=[pltpu.VMEM((devices, ROWS, cells), jnp.float32)] * 2,
         compiler_params=params,
         name="adjoint",
-    )(place, weeks, modeled, shift, scale, held)
+    )(tile_count, place, weeks, modeled, shift, weight, held)
     peak = slots * per_tile * sounds * 0.125 * 3.0 * 1548.0
 
     def swap_sum(value, added, mask):

time: 35 us -> 34.7 us (level)
  no operation moved by 1% of the time
where the time goes in v5:
time: 34.7 us; the launch traced here: 34.3 us
  starting transfers between devices  14.5 us (42%)
  waiting for transfers between devices  10.3 us (30%)
  Pallas kernels  5.85 us (17%)
  other arithmetic  2.21 us (6%)
  between operations  1.39 us (4%)
    ppermute x11, starting transfers between devices, swap(): return lax.ppermute(value, axis, [(i, i ^ mask) for i in range(count)])  14.5 us
    ppermute x11, waiting for transfers between devices, swap(): return lax.ppermute(value, axis, [(i, i ^ mask) for i in range(count)])  10.3 us
    pallas_call x1, Pallas kernels, on_device(): pl.pallas_call(functools.partial(prepare_kernel, rounds), out_shape=(shap...  2.35 us
    pallas_call x1, Pallas kernels, on_device(): pl.pallas_call(forward_kernel, out_shape=shape((slots, MEMBERS, sounds),...  1.91 us
    pallas_call x1, Pallas kernels, on_device(): pl.pallas_call(adjoint_kernel, out_shape=(shape((half, ROWS, cells), jnp....  1.59 us
    concatenate x1, other arithmetic, on_device(): jnp.concatenate([have] * (len(masks) + 1), axis=0)  0.79 us
  transfers between devices with their start and end apart: 11, of which 8 were waited for; matrix products, arithmetic and copies ran while one was open for 4% of the time, Pallas kernels for 7%

profile of v5, /device:TPU:0, one launch (start us, length us, event | category | flops | bytes accessed | tf_op | source)
XLA Modules:
  0.0 34.3 jit_solution(9287059415633376854)
XLA Ops:
  0.6 3.5 %collective-permute-start = (bf16[1,64,128]{2,1,0:T(8,128)(2,1)}, bf16[1,64,128]{2,1,0:T(8,128)(2,1)S(1)}, u32[]{:S(2)}, u32[]{:S(2)}) collective-permute-start(bf16[1,64,128]{2,1,0:T(8,128)(2,1)} %bitcast.5), channel_id=1, source_target_pairs={{0,18},{2,16},{4,22},{6,20},{8,26},{10,24},{12,30},{14,28},{16,2},... | collective-permute-start | bytes 49160 | tf_op jit(solution)/shard_map/ppermute | solution.py:44
  4.2 0.8 %pad_maximum_fusion = bf16[2,64,128]{2,1,0:T(8,128)(2,1)S(1)} fusion(bf16[1,64,128]{2,1,0:T(8,128)(2,1)} %bitcast.6), kind=kLoop, calls=%fused_computation.16 | loop fusion | flops 16384 | bytes 49152 | tf_op jit(solution)/shard_map/concatenate | solution.py:186
  5.0 0.9 %collective-permute-done = bf16[1,64,128]{2,1,0:T(8,128)(2,1)S(1)} collective-permute-done((bf16[1,64,128]{2,1,0:T(8,128)(2,1)}, bf16[1,64,128]{2,1,0:T(8,128)(2,1)S(1)}, u32[]{:S(2)}, u32[]{:S(2)}) %collective-permute-start) | collective-permute-done | bytes 16416 | tf_op jit(solution)/shard_map/ppermute | solution.py:44
  5.8 1.8 %collective-permute-start.3 = (bf16[2,64,128]{2,1,0:T(8,128)(2,1)S(1)}, bf16[2,64,128]{2,1,0:T(8,128)(2,1)S(1)}, u32[]{:S(2)}, u32[]{:S(2)}) collective-permute-start(bf16[2,64,128]{2,1,0:T(8,128)(2,1)S(1)} %constant_dynamic-update-slice_fusion.4.gate_ref), channel_id=1, source_target_pairs={{0,6},{2,4},{4,2},{6,0},{8,14},{10,12},{12,10},{14,8},{16,22},{18,... | collective-permute-start | bytes 98312 | tf_op jit(solution)/shard_map/ppermute | solution.py:44
  7.6 1.6 %collective-permute-start.2 = (bf16[2,64,128]{2,1,0:T(8,128)(2,1)S(1)}, bf16[2,64,128]{2,1,0:T(8,128)(2,1)S(1)}, u32[]{:S(2)}, u32[]{:S(2)}) collective-permute-start(bf16[2,64,128]{2,1,0:T(8,128)(2,1)S(1)} %constant_dynamic-update-slice_fusion.4.gate_ref), channel_id=1, source_target_pairs={{0,10},{2,8},{4,14},{6,12},{8,2},{10,0},{12,6},{14,4},{16,26},{18,... | collective-permute-start | bytes 98312 | tf_op jit(solution)/shard_map/ppermute | solution.py:44
  9.2 0.1 collective-permute-start.1
  9.3 2.4 %prepare.1 = (s32[8,16]{1,0:T(8,128)S(1)}, s32[16,128]{1,0:T(8,128)S(1)}, f32[16,16,128]{2,1,0:T(8,128)S(1)}, f32[16,128]{1,0:T(8,128)S(1)}, bf16[16,8,128,128]{3,2,1,0:T(8,128)(2,1)S(1)}) custom-call(bf16[2,64,128]{2,1,0:T(8,128)(2,1)S(1)} %constant_dynamic-update-slice_fusion.4.gate_ref, s32[8,16]{1,0:T(8,128)} %bitcast.7, s32[1,16]{1,0:T(1,128)} %bitcast.8, ...), custom_call_target="tpu_custom_call" | custom-call | bytes 8388608 | tf_op jit(solution)/shard_map/prepare/pallas_call | solution.py:199
  11.7 0.0 collective-permute-done.3
  11.7 0.0 collective-permute-done.2
  11.7 1.9 %collective-permute-done.1 = bf16[2,64,128]{2,1,0:T(8,128)(2,1)S(1)} collective-permute-done((bf16[2,64,128]{2,1,0:T(8,128)(2,1)S(1)}, bf16[2,64,128]{2,1,0:T(8,128)(2,1)S(1)}, u32[]{:S(2)}, u32[]{:S(2)}) %collective-permute-start.1) | collective-permute-done | bytes 32800 | tf_op jit(solution)/shard_map/ppermute | solution.py:44
  13.6 0.2 collective-permute-start.4
  13.8 1.2 %collective-permute-done.4.other_ref = bf16[8,64,128]{2,1,0:T(8,128)(2,1)S(1)} collective-permute-done((bf16[8,64,128]{2,1,0:T(8,128)(2,1)S(1)}, bf16[8,64,128]{2,1,0:T(8,128)(2,1)S(1)}, u32[]{:S(2)}, u32[]{:S(2)}) %collective-permute-start.4) | collective-permute-done | bytes 131104 | tf_op jit(solution)/shard_map/ppermute | solution.py:44
  15.0 1.9 %forward.1 = f32[16,16,128]{2,1,0:T(8,128)S(1)} custom-call(s32[8,16]{1,0:T(8,128)S(1)} %get-tuple-element.15.place_ref, s32[16,128]{1,0:T(8,128)S(1)} %get-tuple-element.16.weeks_ref, bf16[8,64,128]{2,1,0:T(8,128)(2,1)S(1)} %constant_dynamic-update-slice_fusion.mine_ref, bf16[8,64,128]{2,1,0:T(8,128)(2,1)S(1)} %collective-permute-done.4.other_ref, ...), custom_call_target="tpu_custom_call" | custom-call | tf_op jit(solution)/shard_map/forward/pallas_call | solution.py:223
  17.0 1.6 %collective-permute-start.5 = (f16[16,16,128]{2,1,0:T(8,128)(2,1)S(1)}, f16[16,16,128]{2,1,0:T(8,128)(2,1)S(1)}, u32[]{:S(2)}, u32[]{:S(2)}) collective-permute-start(f16[16,16,128]{2,1,0:T(8,128)(2,1)S(1)} %convert_element_type.42), channel_id=1, source_target_pairs={{0,1},{1,0},{2,3},{3,2},{4,5},{5,4},{6,7},{7,6},{8,9},{9,8},{10,11... | collective-permute-start | bytes 196616 | tf_op jit(solution)/shard_map/ppermute | solution.py:44
  19.2 2.1 %collective-permute-done.5 = f16[16,16,128]{2,1,0:T(8,128)(2,1)S(1)} collective-permute-done((f16[16,16,128]{2,1,0:T(8,128)(2,1)S(1)}, f16[16,16,128]{2,1,0:T(8,128)(2,1)S(1)}, u32[]{:S(2)}, u32[]{:S(2)}) %collective-permute-start.5) | collective-permute-done | bytes 65568 | tf_op jit(solution)/shard_map/ppermute | solution.py:44
  21.3 1.6 %adjoint.1 = (f32[8,64,128]{2,1,0:T(8,128)S(1)}, f32[8,64,128]{2,1,0:T(8,128)S(1)}, f32[16,16,128]{2,1,0:T(8,128)S(1)}) custom-call(s32[1]{0:T(128)S(6)} %copy.15.count_ref, s32[8,16]{1,0:T(8,128)S(1)} %get-tuple-element.15.place_ref, s32[16,128]{1,0:T(8,128)S(1)} %get-tuple-element.16.weeks_ref, f32[16,16,128]{2,1,0:T(8,128)S(1)} %convert_add_fusion.modeled_ref, ...), custom_call_target="tpu_custom_call" | custom-call | tf_op jit(solution)/shard_map/adjoint/pallas_call | solution.py:239
  23.0 0.1 collective-permute-start.6
  23.0 1.3 %collective-permute-done.6 = f16[8,64,128]{2,1,0:T(8,128)(2,1)S(1)} collective-permute-done((f16[8,64,128]{2,1,0:T(8,128)(2,1)S(1)}, f16[8,64,128]{2,1,0:T(8,128)(2,1)S(1)}, u32[]{:S(2)}, u32[]{:S(2)}) %collective-permute-start.6) | collective-permute-done | bytes 131104 | tf_op jit(solution)/shard_map/ppermute | solution.py:44
  24.4 0.7 %collective-permute-start.7 = (f16[2,64,128]{2,1,0:T(8,128)(2,1)S(1)}, f16[2,64,128]{2,1,0:T(8,128)(2,1)S(1)}, u32[]{:S(2)}, u32[]{:S(2)}) collective-permute-start(f16[2,64,128]{2,1,0:T(8,128)(2,1)S(1)} %get-tuple-element.28), channel_id=1, source_target_pairs={{0,14},{2,12},{4,10},{6,8},{8,6},{10,4},{12,2},{14,0},{16,30},{18,... | collective-permute-start | bytes 98312 | tf_op jit(solution)/shard_map/ppermute | solution.py:44
  25.1 1.0 %collective-permute-start.9 = (f16[2,64,128]{2,1,0:T(8,128)(2,1)S(1)}, f16[2,64,128]{2,1,0:T(8,128)(2,1)S(1)}, u32[]{:S(2)}, u32[]{:S(2)}) collective-permute-start(f16[2,64,128]{2,1,0:T(8,128)(2,1)S(1)} %get-tuple-element.29), channel_id=1, source_target_pairs={{0,6},{2,4},{4,2},{6,0},{8,14},{10,12},{12,10},{14,8},{16,22},{18,... | collective-permute-start | bytes 98312 | tf_op jit(solution)/shard_map/ppermute | solution.py:44
  26.1 1.3 %collective-permute-start.8 = (f16[2,64,128]{2,1,0:T(8,128)(2,1)S(1)}, f16[2,64,128]{2,1,0:T(8,128)(2,1)S(1)}, u32[]{:S(2)}, u32[]{:S(2)}) collective-permute-start(f16[2,64,128]{2,1,0:T(8,128)(2,1)S(1)} %get-tuple-element.30), channel_id=1, source_target_pairs={{0,10},{2,8},{4,14},{6,12},{8,2},{10,0},{12,6},{14,4},{16,26},{18,... | collective-permute-start | bytes 98312 | tf_op jit(solution)/shard_map/ppermute | solution.py:44
  27.5 1.4 %collective-permute-done.7 = f16[2,64,128]{2,1,0:T(8,128)(2,1)S(1)} collective-permute-done((f16[2,64,128]{2,1,0:T(8,128)(2,1)S(1)}, f16[2,64,128]{2,1,0:T(8,128)(2,1)S(1)}, u32[]{:S(2)}, u32[]{:S(2)}) %collective-permute-start.7) | collective-permute-done | bytes 32800 | tf_op jit(solution)/shard_map/ppermute | solution.py:44
  28.9 0.0 collective-permute-done.9
  28.9 0.6 %collective-permute-done.8 = f16[2,64,128]{2,1,0:T(8,128)(2,1)S(1)} collective-permute-done((f16[2,64,128]{2,1,0:T(8,128)(2,1)S(1)}, f16[2,64,128]{2,1,0:T(8,128)(2,1)S(1)}, u32[]{:S(2)}, u32[]{:S(2)}) %collective-permute-start.8) | collective-permute-done | bytes 32800 | tf_op jit(solution)/shard_map/ppermute | solution.py:44
  29.5 2.6 %collective-permute-start.10 = (f16[1,64,128]{2,1,0:T(8,128)(2,1)S(1)}, f16[1,64,128]{2,1,0:T(8,128)(2,1)S(1)}, u32[]{:S(2)}, u32[]{:S(2)}) collective-permute-start(f16[1,64,128]{2,1,0:T(8,128)(2,1)S(1)} %fusion.5), channel_id=1, source_target_pairs={{0,18},{2,16},{4,22},{6,20},{8,26},{10,24},{12,30},{14,28},{16,2},... | collective-permute-start | bytes 49160 | tf_op jit(solution)/shard_map/ppermute | solution.py:44
  32.1 0.6 %convert_element_type.55 = bf16[16,16,128]{2,1,0:T(8,128)(2,1)} convert(f32[16,16,128]{2,1,0:T(8,128)S(1)} %get-tuple-element.27) | non-fusion elementwise | flops 32768 | bytes 196608 | tf_op jit(solution)/shard_map/convert_element_type | solution.py:268
  32.8 0.9 %collective-permute-done.10 = f16[1,64,128]{2,1,0:T(8,128)(2,1)S(1)} collective-permute-done((f16[1,64,128]{2,1,0:T(8,128)(2,1)S(1)}, f16[1,64,128]{2,1,0:T(8,128)(2,1)S(1)}, u32[]{:S(2)}, u32[]{:S(2)}) %collective-permute-start.10) | collective-permute-done | bytes 16416 | tf_op jit(solution)/shard_map/ppermute | solution.py:44
  33.7 0.6 %fusion.6 = f32[1,1,64,128]{3,2,1,0:T(8,128)} fusion(f32[2,64,128]{2,1,0:T(8,128)S(1)} %fusion.4, f16[1,64,128]{2,1,0:T(8,128)(2,1)S(1)} %collective-permute-done.10), kind=kLoop, calls=%fused_computation.15 | loop fusion | flops 24576 | bytes 81920 | tf_op jit(solution)/shard_map/broadcast_in_dim | solution.py:268
  (12 shorter events, 0.2 us)
Async XLA Ops:
  0.6 5.2 %collective-permute-start = (bf16[1,64,128]{2,1,0:T(8,128)(2,1)}, bf16[1,64,128]{2,1,0:T(8,128)(2,1)S(1)}, u32[]{:S(2)}, u32[]{:S(2)}) collective-permute-start(bf16[1,64,128]{2,1,0:T(8,128)(2,1)} %bitcast.5), channel_id=1, source_target_pairs={{0,18},{2,16},{4,22},{6,20},{8,26},{10,24},{12,30},{14,28},{16,2},... | collective-permute-start | bytes 49160 | tf_op jit(solution)/shard_map/ppermute | solution.py:44
  5.8 5.8 %collective-permute-start.3 = (bf16[2,64,128]{2,1,0:T(8,128)(2,1)S(1)}, bf16[2,64,128]{2,1,0:T(8,128)(2,1)S(1)}, u32[]{:S(2)}, u32[]{:S(2)}) collective-permute-start(bf16[2,64,128]{2,1,0:T(8,128)(2,1)S(1)} %constant_dynamic-update-slice_fusion.4.gate_ref), channel_id=1, source_target_pairs={{0,6},{2,4},{4,2},{6,0},{8,14},{10,12},{12,10},{14,8},{16,22},{18,... | collective-permute-start | bytes 98312 | tf_op jit(solution)/shard_map/ppermute | solution.py:44
  7.6 4.0 %collective-permute-start.2 = (bf16[2,64,128]{2,1,0:T(8,128)(2,1)S(1)}, bf16[2,64,128]{2,1,0:T(8,128)(2,1)S(1)}, u32[]{:S(2)}, u32[]{:S(2)}) collective-permute-start(bf16[2,64,128]{2,1,0:T(8,128)(2,1)S(1)} %constant_dynamic-update-slice_fusion.4.gate_ref), channel_id=1, source_target_pairs={{0,10},{2,8},{4,14},{6,12},{8,2},{10,0},{12,6},{14,4},{16,26},{18,... | collective-permute-start | bytes 98312 | tf_op jit(solution)/shard_map/ppermute | solution.py:44
  9.2 4.3 %collective-permute-start.1 = (bf16[2,64,128]{2,1,0:T(8,128)(2,1)S(1)}, bf16[2,64,128]{2,1,0:T(8,128)(2,1)S(1)}, u32[]{:S(2)}, u32[]{:S(2)}) collective-permute-start(bf16[2,64,128]{2,1,0:T(8,128)(2,1)S(1)} %constant_dynamic-update-slice_fusion.4.gate_ref), channel_id=1, source_target_pairs={{0,14},{2,12},{4,10},{6,8},{8,6},{10,4},{12,2},{14,0},{16,30},{18,... | collective-permute-start | bytes 98312 | tf_op jit(solution)/shard_map/ppermute | solution.py:44
  13.6 1.4 %collective-permute-start.4 = (bf16[8,64,128]{2,1,0:T(8,128)(2,1)S(1)}, bf16[8,64,128]{2,1,0:T(8,128)(2,1)S(1)}, u32[]{:S(2)}, u32[]{:S(2)}) collective-permute-start(bf16[8,64,128]{2,1,0:T(8,128)(2,1)S(1)} %constant_dynamic-update-slice_fusion.mine_ref), channel_id=1, source_target_pairs={{0,2},{2,0},{4,6},{6,4},{8,10},{10,8},{12,14},{14,12},{16,18},{18,... | collective-permute-start | bytes 393224 | tf_op jit(solution)/shard_map/ppermute | solution.py:44
  17.0 4.3 %collective-permute-start.5 = (f16[16,16,128]{2,1,0:T(8,128)(2,1)S(1)}, f16[16,16,128]{2,1,0:T(8,128)(2,1)S(1)}, u32[]{:S(2)}, u32[]{:S(2)}) collective-permute-start(f16[16,16,128]{2,1,0:T(8,128)(2,1)S(1)} %convert_element_type.42), channel_id=1, source_target_pairs={{0,1},{1,0},{2,3},{3,2},{4,5},{5,4},{6,7},{7,6},{8,9},{9,8},{10,11... | collective-permute-start | bytes 196616 | tf_op jit(solution)/shard_map/ppermute | solution.py:44
  23.0 1.4 %collective-permute-start.6 = (f16[8,64,128]{2,1,0:T(8,128)(2,1)S(1)}, f16[8,64,128]{2,1,0:T(8,128)(2,1)S(1)}, u32[]{:S(2)}, u32[]{:S(2)}) collective-permute-start(f16[8,64,128]{2,1,0:T(8,128)(2,1)S(1)} %multiply_convert_fusion), channel_id=1, source_target_pairs={{0,2},{2,0},{4,6},{6,4},{8,10},{10,8},{12,14},{14,12},{16,18},{18,... | collective-permute-start | bytes 393224 | tf_op jit(solution)/shard_map/ppermute | solution.py:44
  24.4 4.4 %collective-permute-start.7 = (f16[2,64,128]{2,1,0:T(8,128)(2,1)S(1)}, f16[2,64,128]{2,1,0:T(8,128)(2,1)S(1)}, u32[]{:S(2)}, u32[]{:S(2)}) collective-permute-start(f16[2,64,128]{2,1,0:T(8,128)(2,1)S(1)} %get-tuple-element.28), channel_id=1, source_target_pairs={{0,14},{2,12},{4,10},{6,8},{8,6},{10,4},{12,2},{14,0},{16,30},{18,... | collective-permute-start | bytes 98312 | tf_op jit(solution)/shard_map/ppermute | solution.py:44
  25.1 3.7 %collective-permute-start.9 = (f16[2,64,128]{2,1,0:T(8,128)(2,1)S(1)}, f16[2,64,128]{2,1,0:T(8,128)(2,1)S(1)}, u32[]{:S(2)}, u32[]{:S(2)}) collective-permute-start(f16[2,64,128]{2,1,0:T(8,128)(2,1)S(1)} %get-tuple-element.29), channel_id=1, source_target_pairs={{0,6},{2,4},{4,2},{6,0},{8,14},{10,12},{12,10},{14,8},{16,22},{18,... | collective-permute-start | bytes 98312 | tf_op jit(solution)/shard_map/ppermute | solution.py:44
  26.1 3.3 %collective-permute-start.8 = (f16[2,64,128]{2,1,0:T(8,128)(2,1)S(1)}, f16[2,64,128]{2,1,0:T(8,128)(2,1)S(1)}, u32[]{:S(2)}, u32[]{:S(2)}) collective-permute-start(f16[2,64,128]{2,1,0:T(8,128)(2,1)S(1)} %get-tuple-element.30), channel_id=1, source_target_pairs={{0,10},{2,8},{4,14},{6,12},{8,2},{10,0},{12,6},{14,4},{16,26},{18,... | collective-permute-start | bytes 98312 | tf_op jit(solution)/shard_map/ppermute | solution.py:44
  29.5 4.1 %collective-permute-start.10 = (f16[1,64,128]{2,1,0:T(8,128)(2,1)S(1)}, f16[1,64,128]{2,1,0:T(8,128)(2,1)S(1)}, u32[]{:S(2)}, u32[]{:S(2)}) collective-permute-start(f16[1,64,128]{2,1,0:T(8,128)(2,1)S(1)} %fusion.5), channel_id=1, source_target_pairs={{0,18},{2,16},{4,22},{6,20},{8,26},{10,24},{12,30},{14,28},{16,2},... | collective-permute-start | bytes 49160 | tf_op jit(solution)/shard_map/ppermute | solution.py:44

commit v6 on v5

--- a/solution.py
+++ b/solution.py
@@ -63,6 +63,7 @@
     ids_ref,
     seen_ref,
     noise_ref,
+    table_ref,
     sems,
 ):
     pairs = (
@@ -88,7 +89,9 @@
         for mask in masks:
             place = place + jnp.where(low == mask & ~1, order.index(mask), 0)
         odd = odd ^ jnp.where(low != 0, 1, 0)
-    place_ref[...] = place + odd * len(order)
+    table_ref[...] = place + odd * len(order)
+    spread = pltpu.make_async_copy(table_ref, place_ref, sems.at[len(pairs)])
+    spread.start()
     column = lax.broadcasted_iota(jnp.int32, (MEMBERS, MEMBERS), 1)
     row = lax.broadcasted_iota(jnp.int32, (MEMBERS, MEMBERS), 0)
     chosen = jnp.zeros((MEMBERS, MEMBERS), jnp.int32)
@@ -98,6 +101,7 @@
     for tile in range(shift_ref.shape[0]):
         shifted = jnp.dot(hot, noise_ref[tile], preferred_element_type=jnp.float32)
         shift_ref[tile] = seen_ref[pl.ds(tile, 1), :] + shifted
+    spread.wait()
     copies[-1].wait()
 
 
@@ -199,16 +203,16 @@
     place, weeks, shift, weight, held = pl.pallas_call(
         functools.partial(prepare_kernel, rounds),
         out_shape=(
-            shape((per_tile, slots), jnp.int32),
+            pltpu.SMEM((per_tile, slots), jnp.int32),
             shape(sounding_week.shape, jnp.int32),
             shape((slots, MEMBERS, sounds), jnp.float32),
             shape((slots, sounds), jnp.float32),
             shape(footprint.shape, footprint.dtype),
         ),
         in_specs=[VMEM] + [HBM] * 7,
-        out_specs=(VMEM,) * 5,
+        out_specs=(SMEM,) + (VMEM,) * 4,
         scratch_shapes=[kind(x.shape, x.dtype) for x, kind in small if kind]
-        + [pltpu.SemaphoreType.DMA((7,))],
+        + [pltpu.VMEM((per_tile, slots), jnp.int32), pltpu.SemaphoreType.DMA((8,))],
         compiler_params=params,
         cost_estimate=pl.CostEstimate(flops=0, bytes_accessed=2 * footprint.size * 2, transcendentals=0),
         name="prepare",

time: 34.7 us -> 33.4 us (0.963)
  Pallas kernels: 5.85 us -> 4.63 us
    pallas_call x1, Pallas kernels: 1.59 us -> 0.97 us  [on_device(): pl.pallas_call(adjoint_kernel, out_shape=(shape((half, ROWS, cells), jnp....]
    pallas_call x1, Pallas kernels: 1.91 us -> 1.3 us  [on_device(): pl.pallas_call(forward_kernel, out_shape=shape((slots, MEMBERS, sounds),...]
where the time goes in v6:
time: 33.4 us; the launch traced here: 33.1 us
  starting transfers between devices  14.5 us (43%)
  waiting for transfers between devices  10.3 us (31%)
  Pallas kernels  4.63 us (14%)
  other arithmetic  2.21 us (7%)
  between operations  1.39 us (4%)
    ppermute x11, starting transfers between devices, swap(): return lax.ppermute(value, axis, [(i, i ^ mask) for i in range(count)])  14.5 us
    ppermute x11, waiting for transfers between devices, swap(): return lax.ppermute(value, axis, [(i, i ^ mask) for i in range(count)])  10.3 us
    pallas_call x1, Pallas kernels, on_device(): pl.pallas_call(functools.partial(prepare_kernel, rounds), out_shape=(pltp...  2.36 us
    pallas_call x1, Pallas kernels, on_device(): pl.pallas_call(forward_kernel, out_shape=shape((slots, MEMBERS, sounds),...  1.3 us
    pallas_call x1, Pallas kernels, on_device(): pl.pallas_call(adjoint_kernel, out_shape=(shape((half, ROWS, cells), jnp....  0.97 us
    concatenate x1, other arithmetic, on_device(): jnp.concatenate([have] * (len(masks) + 1), axis=0)  0.79 us
  transfers between devices with their start and end apart: 11, of which 8 were waited for; matrix products, arithmetic and copies ran while one was open for 4% of the time, Pallas kernels for 7%

profile of v6, /device:TPU:0, one launch (start us, length us, event | category | flops | bytes accessed | tf_op | source)
XLA Modules:
  0.0 33.1 jit_solution(7100512588319395847)
XLA Ops:
  0.6 3.5 %collective-permute-start = (bf16[1,64,128]{2,1,0:T(8,128)(2,1)}, bf16[1,64,128]{2,1,0:T(8,128)(2,1)S(1)}, u32[]{:S(2)}, u32[]{:S(2)}) collective-permute-start(bf16[1,64,128]{2,1,0:T(8,128)(2,1)} %bitcast.5), channel_id=1, source_target_pairs={{0,18},{2,16},{4,22},{6,20},{8,26},{10,24},{12,30},{14,28},{16,2},... | collective-permute-start | bytes 49160 | tf_op jit(solution)/shard_map/ppermute | solution.py:44
  4.2 0.8 %pad_maximum_fusion = bf16[2,64,128]{2,1,0:T(8,128)(2,1)S(1)} fusion(bf16[1,64,128]{2,1,0:T(8,128)(2,1)} %bitcast.6), kind=kLoop, calls=%fused_computation.16 | loop fusion | flops 16384 | bytes 49152 | tf_op jit(solution)/shard_map/concatenate | solution.py:190
  5.0 0.9 %collective-permute-done = bf16[1,64,128]{2,1,0:T(8,128)(2,1)S(1)} collective-permute-done((bf16[1,64,128]{2,1,0:T(8,128)(2,1)}, bf16[1,64,128]{2,1,0:T(8,128)(2,1)S(1)}, u32[]{:S(2)}, u32[]{:S(2)}) %collective-permute-start) | collective-permute-done | bytes 16416 | tf_op jit(solution)/shard_map/ppermute | solution.py:44
  5.8 1.8 %collective-permute-start.3 = (bf16[2,64,128]{2,1,0:T(8,128)(2,1)S(1)}, bf16[2,64,128]{2,1,0:T(8,128)(2,1)S(1)}, u32[]{:S(2)}, u32[]{:S(2)}) collective-permute-start(bf16[2,64,128]{2,1,0:T(8,128)(2,1)S(1)} %constant_dynamic-update-slice_fusion.4.gate_ref), channel_id=1, source_target_pairs={{0,6},{2,4},{4,2},{6,0},{8,14},{10,12},{12,10},{14,8},{16,22},{18,... | collective-permute-start | bytes 98312 | tf_op jit(solution)/shard_map/ppermute | solution.py:44
  7.6 1.6 %collective-permute-start.2 = (bf16[2,64,128]{2,1,0:T(8,128)(2,1)S(1)}, bf16[2,64,128]{2,1,0:T(8,128)(2,1)S(1)}, u32[]{:S(2)}, u32[]{:S(2)}) collective-permute-start(bf16[2,64,128]{2,1,0:T(8,128)(2,1)S(1)} %constant_dynamic-update-slice_fusion.4.gate_ref), channel_id=1, source_target_pairs={{0,10},{2,8},{4,14},{6,12},{8,2},{10,0},{12,6},{14,4},{16,26},{18,... | collective-permute-start | bytes 98312 | tf_op jit(solution)/shard_map/ppermute | solution.py:44
  9.2 0.1 collective-permute-start.1
  9.3 2.4 %prepare.1 = (s32[8,16]{1,0:T(8,128)S(4)}, s32[16,128]{1,0:T(8,128)S(1)}, f32[16,16,128]{2,1,0:T(8,128)S(1)}, f32[16,128]{1,0:T(8,128)S(1)}, bf16[16,8,128,128]{3,2,1,0:T(8,128)(2,1)S(1)}) custom-call(bf16[2,64,128]{2,1,0:T(8,128)(2,1)S(1)} %constant_dynamic-update-slice_fusion.4.gate_ref, s32[8,16]{1,0:T(8,128)} %bitcast.7, s32[1,16]{1,0:T(1,128)} %bitcast.8, ...), custom_call_target="tpu_custom_call" | custom-call | bytes 8388608 | tf_op jit(solution)/shard_map/prepare/pallas_call | solution.py:203
  11.7 0.0 collective-permute-done.3
  11.7 0.0 collective-permute-done.2
  11.7 1.9 %collective-permute-done.1 = bf16[2,64,128]{2,1,0:T(8,128)(2,1)S(1)} collective-permute-done((bf16[2,64,128]{2,1,0:T(8,128)(2,1)S(1)}, bf16[2,64,128]{2,1,0:T(8,128)(2,1)S(1)}, u32[]{:S(2)}, u32[]{:S(2)}) %collective-permute-start.1) | collective-permute-done | bytes 32800 | tf_op jit(solution)/shard_map/ppermute | solution.py:44
  13.6 0.2 collective-permute-start.4
  13.8 1.2 %collective-permute-done.4.other_ref = bf16[8,64,128]{2,1,0:T(8,128)(2,1)S(1)} collective-permute-done((bf16[8,64,128]{2,1,0:T(8,128)(2,1)S(1)}, bf16[8,64,128]{2,1,0:T(8,128)(2,1)S(1)}, u32[]{:S(2)}, u32[]{:S(2)}) %collective-permute-start.4) | collective-permute-done | bytes 131104 | tf_op jit(solution)/shard_map/ppermute | solution.py:44
  15.0 1.3 %forward.1 = f32[16,16,128]{2,1,0:T(8,128)S(1)} custom-call(s32[8,16]{1,0:T(8,128)S(4)} %get-tuple-element.15.place_ref, s32[16,128]{1,0:T(8,128)S(1)} %get-tuple-element.16.weeks_ref, bf16[8,64,128]{2,1,0:T(8,128)(2,1)S(1)} %constant_dynamic-update-slice_fusion.mine_ref, bf16[8,64,128]{2,1,0:T(8,128)(2,1)S(1)} %collective-permute-done.4.other_ref, ...), custom_call_target="tpu_custom_call" | custom-call | tf_op jit(solution)/shard_map/forward/pallas_call | solution.py:227
  16.4 1.6 %collective-permute-start.5 = (f16[16,16,128]{2,1,0:T(8,128)(2,1)S(1)}, f16[16,16,128]{2,1,0:T(8,128)(2,1)S(1)}, u32[]{:S(2)}, u32[]{:S(2)}) collective-permute-start(f16[16,16,128]{2,1,0:T(8,128)(2,1)S(1)} %convert_element_type.42), channel_id=1, source_target_pairs={{0,1},{1,0},{2,3},{3,2},{4,5},{5,4},{6,7},{7,6},{8,9},{9,8},{10,11... | collective-permute-start | bytes 196616 | tf_op jit(solution)/shard_map/ppermute | solution.py:44
  18.6 2.1 %collective-permute-done.5 = f16[16,16,128]{2,1,0:T(8,128)(2,1)S(1)} collective-permute-done((f16[16,16,128]{2,1,0:T(8,128)(2,1)S(1)}, f16[16,16,128]{2,1,0:T(8,128)(2,1)S(1)}, u32[]{:S(2)}, u32[]{:S(2)}) %collective-permute-start.5) | collective-permute-done | bytes 65568 | tf_op jit(solution)/shard_map/ppermute | solution.py:44
  20.7 1.0 %adjoint.1 = (f32[8,64,128]{2,1,0:T(8,128)S(1)}, f32[8,64,128]{2,1,0:T(8,128)S(1)}, f32[16,16,128]{2,1,0:T(8,128)S(1)}) custom-call(s32[1]{0:T(128)S(6)} %copy.15.count_ref, s32[8,16]{1,0:T(8,128)S(4)} %get-tuple-element.15.place_ref, s32[16,128]{1,0:T(8,128)S(1)} %get-tuple-element.16.weeks_ref, f32[16,16,128]{2,1,0:T(8,128)S(1)} %convert_add_fusion.modeled_ref, ...), custom_call_target="tpu_custom_call" | custom-call | tf_op jit(solution)/shard_map/adjoint/pallas_call | solution.py:243
  21.7 0.1 collective-permute-start.6
  21.8 1.3 %collective-permute-done.6 = f16[8,64,128]{2,1,0:T(8,128)(2,1)S(1)} collective-permute-done((f16[8,64,128]{2,1,0:T(8,128)(2,1)S(1)}, f16[8,64,128]{2,1,0:T(8,128)(2,1)S(1)}, u32[]{:S(2)}, u32[]{:S(2)}) %collective-permute-start.6) | collective-permute-done | bytes 131104 | tf_op jit(solution)/shard_map/ppermute | solution.py:44
  23.2 0.7 %collective-permute-start.7 = (f16[2,64,128]{2,1,0:T(8,128)(2,1)S(1)}, f16[2,64,128]{2,1,0:T(8,128)(2,1)S(1)}, u32[]{:S(2)}, u32[]{:S(2)}) collective-permute-start(f16[2,64,128]{2,1,0:T(8,128)(2,1)S(1)} %get-tuple-element.28), channel_id=1, source_target_pairs={{0,14},{2,12},{4,10},{6,8},{8,6},{10,4},{12,2},{14,0},{16,30},{18,... | collective-permute-start | bytes 98312 | tf_op jit(solution)/shard_map/ppermute | solution.py:44
  23.9 1.0 %collective-permute-start.9 = (f16[2,64,128]{2,1,0:T(8,128)(2,1)S(1)}, f16[2,64,128]{2,1,0:T(8,128)(2,1)S(1)}, u32[]{:S(2)}, u32[]{:S(2)}) collective-permute-start(f16[2,64,128]{2,1,0:T(8,128)(2,1)S(1)} %get-tuple-element.29), channel_id=1, source_target_pairs={{0,6},{2,4},{4,2},{6,0},{8,14},{10,12},{12,10},{14,8},{16,22},{18,... | collective-permute-start | bytes 98312 | tf_op jit(solution)/shard_map/ppermute | solution.py:44
  24.9 1.3 %collective-permute-start.8 = (f16[2,64,128]{2,1,0:T(8,128)(2,1)S(1)}, f16[2,64,128]{2,1,0:T(8,128)(2,1)S(1)}, u32[]{:S(2)}, u32[]{:S(2)}) collective-permute-start(f16[2,64,128]{2,1,0:T(8,128)(2,1)S(1)} %get-tuple-element.30), channel_id=1, source_target_pairs={{0,10},{2,8},{4,14},{6,12},{8,2},{10,0},{12,6},{14,4},{16,26},{18,... | collective-permute-start | bytes 98312 | tf_op jit(solution)/shard_map/ppermute | solution.py:44
  26.3 1.4 %collective-permute-done.7 = f16[2,64,128]{2,1,0:T(8,128)(2,1)S(1)} collective-permute-done((f16[2,64,128]{2,1,0:T(8,128)(2,1)S(1)}, f16[2,64,128]{2,1,0:T(8,128)(2,1)S(1)}, u32[]{:S(2)}, u32[]{:S(2)}) %collective-permute-start.7) | collective-permute-done | bytes 32800 | tf_op jit(solution)/shard_map/ppermute | solution.py:44
  27.6 0.0 collective-permute-done.9
  27.6 0.6 %collective-permute-done.8 = f16[2,64,128]{2,1,0:T(8,128)(2,1)S(1)} collective-permute-done((f16[2,64,128]{2,1,0:T(8,128)(2,1)S(1)}, f16[2,64,128]{2,1,0:T(8,128)(2,1)S(1)}, u32[]{:S(2)}, u32[]{:S(2)}) %collective-permute-start.8) | collective-permute-done | bytes 32800 | tf_op jit(solution)/shard_map/ppermute | solution.py:44
  28.3 2.6 %collective-permute-start.10 = (f16[1,64,128]{2,1,0:T(8,128)(2,1)S(1)}, f16[1,64,128]{2,1,0:T(8,128)(2,1)S(1)}, u32[]{:S(2)}, u32[]{:S(2)}) collective-permute-start(f16[1,64,128]{2,1,0:T(8,128)(2,1)S(1)} %fusion.5), channel_id=1, source_target_pairs={{0,18},{2,16},{4,22},{6,20},{8,26},{10,24},{12,30},{14,28},{16,2},... | collective-permute-start | bytes 49160 | tf_op jit(solution)/shard_map/ppermute | solution.py:44
  30.9 0.6 %convert_element_type.55 = bf16[16,16,128]{2,1,0:T(8,128)(2,1)} convert(f32[16,16,128]{2,1,0:T(8,128)S(1)} %get-tuple-element.27) | non-fusion elementwise | flops 32768 | bytes 196608 | tf_op jit(solution)/shard_map/convert_element_type | solution.py:272
  31.6 0.9 %collective-permute-done.10 = f16[1,64,128]{2,1,0:T(8,128)(2,1)S(1)} collective-permute-done((f16[1,64,128]{2,1,0:T(8,128)(2,1)S(1)}, f16[1,64,128]{2,1,0:T(8,128)(2,1)S(1)}, u32[]{:S(2)}, u32[]{:S(2)}) %collective-permute-start.10) | collective-permute-done | bytes 16416 | tf_op jit(solution)/shard_map/ppermute | solution.py:44
  32.4 0.6 %fusion.6 = f32[1,1,64,128]{3,2,1,0:T(8,128)} fusion(f32[2,64,128]{2,1,0:T(8,128)S(1)} %fusion.4, f16[1,64,128]{2,1,0:T(8,128)(2,1)S(1)} %collective-permute-done.10), kind=kLoop, calls=%fused_computation.15 | loop fusion | flops 24576 | bytes 81920 | tf_op jit(solution)/shard_map/broadcast_in_dim | solution.py:272
  (12 shorter events, 0.2 us)
Async XLA Ops:
  0.6 5.2 %collective-permute-start = (bf16[1,64,128]{2,1,0:T(8,128)(2,1)}, bf16[1,64,128]{2,1,0:T(8,128)(2,1)S(1)}, u32[]{:S(2)}, u32[]{:S(2)}) collective-permute-start(bf16[1,64,128]{2,1,0:T(8,128)(2,1)} %bitcast.5), channel_id=1, source_target_pairs={{0,18},{2,16},{4,22},{6,20},{8,26},{10,24},{12,30},{14,28},{16,2},... | collective-permute-start | bytes 49160 | tf_op jit(solution)/shard_map/ppermute | solution.py:44
  5.8 5.8 %collective-permute-start.3 = (bf16[2,64,128]{2,1,0:T(8,128)(2,1)S(1)}, bf16[2,64,128]{2,1,0:T(8,128)(2,1)S(1)}, u32[]{:S(2)}, u32[]{:S(2)}) collective-permute-start(bf16[2,64,128]{2,1,0:T(8,128)(2,1)S(1)} %constant_dynamic-update-slice_fusion.4.gate_ref), channel_id=1, source_target_pairs={{0,6},{2,4},{4,2},{6,0},{8,14},{10,12},{12,10},{14,8},{16,22},{18,... | collective-permute-start | bytes 98312 | tf_op jit(solution)/shard_map/ppermute | solution.py:44
  7.6 4.0 %collective-permute-start.2 = (bf16[2,64,128]{2,1,0:T(8,128)(2,1)S(1)}, bf16[2,64,128]{2,1,0:T(8,128)(2,1)S(1)}, u32[]{:S(2)}, u32[]{:S(2)}) collective-permute-start(bf16[2,64,128]{2,1,0:T(8,128)(2,1)S(1)} %constant_dynamic-update-slice_fusion.4.gate_ref), channel_id=1, source_target_pairs={{0,10},{2,8},{4,14},{6,12},{8,2},{10,0},{12,6},{14,4},{16,26},{18,... | collective-permute-start | bytes 98312 | tf_op jit(solution)/shard_map/ppermute | solution.py:44
  9.2 4.3 %collective-permute-start.1 = (bf16[2,64,128]{2,1,0:T(8,128)(2,1)S(1)}, bf16[2,64,128]{2,1,0:T(8,128)(2,1)S(1)}, u32[]{:S(2)}, u32[]{:S(2)}) collective-permute-start(bf16[2,64,128]{2,1,0:T(8,128)(2,1)S(1)} %constant_dynamic-update-slice_fusion.4.gate_ref), channel_id=1, source_target_pairs={{0,14},{2,12},{4,10},{6,8},{8,6},{10,4},{12,2},{14,0},{16,30},{18,... | collective-permute-start | bytes 98312 | tf_op jit(solution)/shard_map/ppermute | solution.py:44
  13.6 1.4 %collective-permute-start.4 = (bf16[8,64,128]{2,1,0:T(8,128)(2,1)S(1)}, bf16[8,64,128]{2,1,0:T(8,128)(2,1)S(1)}, u32[]{:S(2)}, u32[]{:S(2)}) collective-permute-start(bf16[8,64,128]{2,1,0:T(8,128)(2,1)S(1)} %constant_dynamic-update-slice_fusion.mine_ref), channel_id=1, source_target_pairs={{0,2},{2,0},{4,6},{6,4},{8,10},{10,8},{12,14},{14,12},{16,18},{18,... | collective-permute-start | bytes 393224 | tf_op jit(solution)/shard_map/ppermute | solution.py:44
  16.4 4.3 %collective-permute-start.5 = (f16[16,16,128]{2,1,0:T(8,128)(2,1)S(1)}, f16[16,16,128]{2,1,0:T(8,128)(2,1)S(1)}, u32[]{:S(2)}, u32[]{:S(2)}) collective-permute-start(f16[16,16,128]{2,1,0:T(8,128)(2,1)S(1)} %convert_element_type.42), channel_id=1, source_target_pairs={{0,1},{1,0},{2,3},{3,2},{4,5},{5,4},{6,7},{7,6},{8,9},{9,8},{10,11... | collective-permute-start | bytes 196616 | tf_op jit(solution)/shard_map/ppermute | solution.py:44
  21.7 1.4 %collective-permute-start.6 = (f16[8,64,128]{2,1,0:T(8,128)(2,1)S(1)}, f16[8,64,128]{2,1,0:T(8,128)(2,1)S(1)}, u32[]{:S(2)}, u32[]{:S(2)}) collective-permute-start(f16[8,64,128]{2,1,0:T(8,128)(2,1)S(1)} %multiply_convert_fusion), channel_id=1, source_target_pairs={{0,2},{2,0},{4,6},{6,4},{8,10},{10,8},{12,14},{14,12},{16,18},{18,... | collective-permute-start | bytes 393224 | tf_op jit(solution)/shard_map/ppermute | solution.py:44
  23.2 4.4 %collective-permute-start.7 = (f16[2,64,128]{2,1,0:T(8,128)(2,1)S(1)}, f16[2,64,128]{2,1,0:T(8,128)(2,1)S(1)}, u32[]{:S(2)}, u32[]{:S(2)}) collective-permute-start(f16[2,64,128]{2,1,0:T(8,128)(2,1)S(1)} %get-tuple-element.28), channel_id=1, source_target_pairs={{0,14},{2,12},{4,10},{6,8},{8,6},{10,4},{12,2},{14,0},{16,30},{18,... | collective-permute-start | bytes 98312 | tf_op jit(solution)/shard_map/ppermute | solution.py:44
  23.9 3.7 %collective-permute-start.9 = (f16[2,64,128]{2,1,0:T(8,128)(2,1)S(1)}, f16[2,64,128]{2,1,0:T(8,128)(2,1)S(1)}, u32[]{:S(2)}, u32[]{:S(2)}) collective-permute-start(f16[2,64,128]{2,1,0:T(8,128)(2,1)S(1)} %get-tuple-element.29), channel_id=1, source_target_pairs={{0,6},{2,4},{4,2},{6,0},{8,14},{10,12},{12,10},{14,8},{16,22},{18,... | collective-permute-start | bytes 98312 | tf_op jit(solution)/shard_map/ppermute | solution.py:44
  24.9 3.3 %collective-permute-start.8 = (f16[2,64,128]{2,1,0:T(8,128)(2,1)S(1)}, f16[2,64,128]{2,1,0:T(8,128)(2,1)S(1)}, u32[]{:S(2)}, u32[]{:S(2)}) collective-permute-start(f16[2,64,128]{2,1,0:T(8,128)(2,1)S(1)} %get-tuple-element.30), channel_id=1, source_target_pairs={{0,10},{2,8},{4,14},{6,12},{8,2},{10,0},{12,6},{14,4},{16,26},{18,... | collective-permute-start | bytes 98312 | tf_op jit(solution)/shard_map/ppermute | solution.py:44
  28.3 4.1 %collective-permute-start.10 = (f16[1,64,128]{2,1,0:T(8,128)(2,1)S(1)}, f16[1,64,128]{2,1,0:T(8,128)(2,1)S(1)}, u32[]{:S(2)}, u32[]{:S(2)}) collective-permute-start(f16[1,64,128]{2,1,0:T(8,128)(2,1)S(1)} %fusion.5), channel_id=1, source_target_pairs={{0,18},{2,16},{4,22},{6,20},{8,26},{10,24},{12,30},{14,28},{16,2},... | collective-permute-start | bytes 49160 | tf_op jit(solution)/shard_map/ppermute | solution.py:44
